TPU v7x, 512 devices: a whole 4x8x8 slice. The times are simulated.
512 devices in a mesh: gx: 2 (over core), ha: 256 (over z, y, x).
Axes of the slice: x: 4, y: 8, z: 8, core: 2. Of those that a mesh axis runs over, the one named last changes fastest.
Arguments:
- level_set: float32 [768, 160, 256], P('ha', 'gx'), may hold values from -6 to 6
- step_length: float32 [1], replicated, may hold values from 0.12 to 0.2
Outputs:
- level_next: float32 [768, 160, 256], P('ha', 'gx')
All inputs are finite; a program needn't handle non-finite values.
Results may differ from a plain program's by a relative error of at most 0.00002.
Values sent between devices are 32-bit elements; how exact they have to be, the bound alone decides.
No kernel may reach another device: no remote copies, remote signals or barrier semaphores. Data moves between devices by JAX's collectives and lax.ppermute only.
A program may use at most 64 MiB of HBM per device.

v0:
```python
import jax
import jax.numpy as jnp
from jax import lax
from jax.sharding import PartitionSpec as P

epsilon_weno = 1e-06
speed_rate = 1.0
turn_rate = 1.0


def extended_2(cells, sides, width, closed):
    for axis, dim in sides:
        count = lax.axis_size(axis)
        ends = count if closed else count - 1
        head = lax.slice_in_dim(cells, 0, width, axis=dim)
        tail = lax.slice_in_dim(cells, cells.shape[dim] - width, cells.shape[dim], axis=dim)
        cells = jnp.concatenate(
            [
                lax.ppermute(tail, axis, [(i, (i + 1) % count) for i in range(ends)]),
                cells,
                lax.ppermute(head, axis, [((i + 1) % count, i) for i in range(ends)]),
            ],
            axis=dim,
        )
    return cells


def weno_blend(slope_one, slope_two, slope_three, slope_four, slope_five):
    guess_one = slope_one / 3.0 - 7.0 * slope_two / 6.0 + 11.0 * slope_three / 6.0
    guess_two = -slope_two / 6.0 + 5.0 * slope_three / 6.0 + slope_four / 3.0
    guess_three = slope_three / 3.0 + 5.0 * slope_four / 6.0 - slope_five / 6.0
    smooth_one = (
        13.0 / 12.0 * (slope_one - 2.0 * slope_two + slope_three) ** 2
        + 0.25 * (slope_one - 4.0 * slope_two + 3.0 * slope_three) ** 2
    )
    smooth_two = (
        13.0 / 12.0 * (slope_two - 2.0 * slope_three + slope_four) ** 2
        + 0.25 * (slope_two - slope_four) ** 2
    )
    smooth_three = (
        13.0 / 12.0 * (slope_three - 2.0 * slope_four + slope_five) ** 2
        + 0.25 * (3.0 * slope_three - 4.0 * slope_four + slope_five) ** 2
    )
    weight_one = 0.1 / (smooth_one + epsilon_weno) ** 2
    weight_two = 0.6 / (smooth_two + epsilon_weno) ** 2
    weight_three = 0.3 / (smooth_three + epsilon_weno) ** 2
    weight_sum = weight_one + weight_two + weight_three
    return (
        weight_one * guess_one + weight_two * guess_two + weight_three * guess_three
    ) / weight_sum


def one_sided(padded, axis, count):
    forward_diff = lax.slice_in_dim(padded, 1, count + 6, axis=axis) - lax.slice_in_dim(
        padded, 0, count + 5, axis=axis
    )
    pieces = [
        lax.slice_in_dim(forward_diff, offset, offset + count, axis=axis) for offset in range(6)
    ]
    minus_side = weno_blend(pieces[0], pieces[1], pieces[2], pieces[3], pieces[4])
    plus_side = weno_blend(pieces[5], pieces[4], pieces[3], pieces[2], pieces[1])
    return (minus_side, plus_side)


def combine_rate(minus_x, plus_x, minus_h, plus_h, minus_y, plus_y, cosine_table, sine_table):
    cos_grid = cosine_table[None, :, None]
    sin_grid = sine_table[None, :, None]
    hamilton = speed_rate * (
        cos_grid * (minus_x + plus_x) * 0.5 + sin_grid * (minus_y + plus_y) * 0.5
    ) - turn_rate * jnp.abs((minus_h + plus_h) * 0.5)
    damping = 0.5 * (
        speed_rate * jnp.abs(cos_grid) * (plus_x - minus_x)
        + speed_rate * jnp.abs(sin_grid) * (plus_y - minus_y)
        + turn_rate * (plus_h - minus_h)
    )
    return damping - jnp.maximum(0.0, -hamilton)


def hamilton_rate(padded, cosine_table, sine_table):
    rows_x = padded.shape[0] - 6
    rows_h = padded.shape[1] - 6
    rows_y = padded.shape[2] - 6
    minus_x, plus_x = one_sided(padded[:, 3:-3, 3:-3], 0, rows_x)
    minus_h, plus_h = one_sided(padded[3:-3, :, 3:-3], 1, rows_h)
    minus_y, plus_y = one_sided(padded[3:-3, 3:-3, :], 2, rows_y)
    return combine_rate(minus_x, plus_x, minus_h, plus_h, minus_y, plus_y, cosine_table, sine_table)


def heading_tables(rows_h):
    total_h = lax.axis_size("gx") * rows_h
    global_h = lax.axis_index("gx") * rows_h + jnp.arange(rows_h, dtype=jnp.int32)
    heading = 2.0 * jnp.pi * global_h.astype(jnp.float32) / total_h
    return (jnp.cos(heading), jnp.sin(heading))


def pad_sides(extended):
    return jnp.pad(extended, ((0, 0), (0, 0), (3, 3)))


def on_device(level_set, step_length):
    step_size = step_length[0]
    rows_h = level_set.shape[1]
    cosine_table, sine_table = heading_tables(rows_h)

    def section_rate(section_field):
        widened = extended_2(section_field, (("ha", 0),), 3, False)
        extended = extended_2(widened, (("gx", 1),), 3, True)
        return hamilton_rate(pad_sides(extended), cosine_table, sine_table)

    section_one = level_set + step_size * section_rate(level_set)
    section_two = 0.75 * level_set + 0.25 * (section_one + step_size * section_rate(section_one))
    return level_set / 3.0 + 2.0 / 3.0 * (section_two + step_size * section_rate(section_two))


def solution(mesh):
    return jax.shard_map(
        on_device,
        mesh=mesh,
        in_specs=(P("ha", "gx", None), P()),
        out_specs=P("ha", "gx", None),
        check_vma=False,
    )
```

profile of v0, /device:TPU:257, one launch (start us, length us, event | category | flops | bytes accessed | tf_op | source)
XLA Modules:
  0.0 88.4 jit_solution(13552806992186038947)
XLA Ops:
  0.0 3.1 %collective-permute-start = (f32[3,80,256]{2,1,0:T(8,128)}, f32[3,80,256]{2,1,0:T(8,128)S(1)}, u32[]{:S(2)}, u32[]{:S(2)}) collective-permute-start(f32[3,80,256]{2,1,0:T(8,128)} %param.2), channel_id=1, source_target_pairs={{0,1},{1,2},{2,3},{3,4},{4,5},{5,6},{6,7},{7,8},{8,9},{9,10},{10,1... | collective-permute-start | bytes 737288 | tf_op jit(solution)/shard_map/ppermute | solution.py:19
  3.1 7.6 %collective-permute-start.1 = (f32[3,80,256]{2,1,0:T(8,128)}, f32[3,80,256]{2,1,0:T(8,128)S(1)}, u32[]{:S(2)}, u32[]{:S(2)}) collective-permute-start(f32[3,80,256]{2,1,0:T(8,128)} %param.2), channel_id=1, source_target_pairs={{1,0},{2,1},{3,2},{4,3},{5,4},{6,5},{7,6},{8,7},{9,8},{10,9},{11,1... | collective-permute-start | bytes 737288 | tf_op jit(solution)/shard_map/ppermute | solution.py:21
  11.5 2.9 %collective-permute-done = f32[3,80,256]{2,1,0:T(8,128)S(1)} collective-permute-done((f32[3,80,256]{2,1,0:T(8,128)}, f32[3,80,256]{2,1,0:T(8,128)S(1)}, u32[]{:S(2)}, u32[]{:S(2)}) %collective-permute-start) | collective-permute-done | bytes 245792 | tf_op jit(solution)/shard_map/ppermute | solution.py:19
  14.4 1.0 %constant_dynamic-update-slice_fusion.1 = f32[9,80,256]{2,1,0:T(8,128)S(1)} fusion(f32[9,80,256]{2,1,0:T(8,128)S(1)} %constant_dynamic-update-slice_fusion.2, f32[3,80,256]{2,1,0:T(8,128)} %param.2), kind=kLoop, calls=%fused_computation.28 | loop fusion | bytes 491520
  15.4 0.0 collective-permute-done.1
  15.4 3.7 %collective-permute-start.3 = (f32[9,3,256]{2,1,0:T(4,128)S(1)}, f32[9,3,256]{2,1,0:T(4,128)S(1)}, u32[]{:S(2)}, u32[]{:S(2)}) collective-permute-start(f32[9,3,256]{2,1,0:T(4,128)S(1)} %get-tuple-element.10), channel_id=1, source_target_pairs={{256,0},{0,256},{257,1},{1,257},{258,2},{2,258},{259,3},{3,259},{2... | collective-permute-start | bytes 82952 | tf_op jit(solution)/shard_map/ppermute | solution.py:21
  19.1 1.9 %collective-permute-start.2 = (f32[9,3,256]{2,1,0:T(4,128)S(1)}, f32[9,3,256]{2,1,0:T(4,128)S(1)}, u32[]{:S(2)}, u32[]{:S(2)}) collective-permute-start(f32[9,3,256]{2,1,0:T(4,128)S(1)} %get-tuple-element.9), channel_id=1, source_target_pairs={{0,256},{256,0},{1,257},{257,1},{2,258},{258,2},{3,259},{259,3},{4... | collective-permute-start | bytes 82952 | tf_op jit(solution)/shard_map/ppermute | solution.py:19
  21.1 0.1 slice_subtract_fusion.2
  21.1 0.0 collective-permute-done.3
  21.1 1.1 %collective-permute-done.2 = f32[9,3,256]{2,1,0:T(4,128)S(1)} collective-permute-done((f32[9,3,256]{2,1,0:T(4,128)S(1)}, f32[9,3,256]{2,1,0:T(4,128)S(1)}, u32[]{:S(2)}, u32[]{:S(2)}) %collective-permute-start.2) | collective-permute-done | bytes 27680 | tf_op jit(solution)/shard_map/ppermute | solution.py:19
  22.3 0.1 pad_maximum_fusion
  22.3 0.0 copy-start
  22.4 0.3 fusion
  22.6 0.6 copy-done
  23.3 3.6 %multiply_add_fusion.2 = f32[3,80,256]{2,1,0:T(8,128)S(1)} fusion(f32[3,80,256]{2,1,0:T(8,128)S(1)} %copy-done, f32[3,85,256]{2,1,0:T(8,128)S(1)} %slice_subtract_fusion.5, f32[3,80,261]{2,1,0:T(8,128)S(1)} %fusion, f32[8,80,256]{2,1,0:T(8,128)S(1)} %slice_subtract_fusion.2, f32[80]{0:T(128)S(1)} %get-tuple-element.11, f32[80]{0:T(128)S(1)} %get-tuple-element.12, ...), kind=kLoop, calls=%fused_computation.22 | loop fusion | flops 24268800 | bytes 4916484 | tf_op jit(solution)/shard_map/add | solution.py:110
  26.9 9.4 %collective-permute-start.5 = (f32[3,80,256]{2,1,0:T(8,128)S(1)}, f32[3,80,256]{2,1,0:T(8,128)S(1)}, u32[]{:S(2)}, u32[]{:S(2)}) collective-permute-start(f32[3,80,256]{2,1,0:T(8,128)S(1)} %multiply_add_fusion.2), channel_id=1, source_target_pairs={{1,0},{2,1},{3,2},{4,3},{5,4},{6,5},{7,6},{8,7},{9,8},{10,9},{11,1... | collective-permute-start | bytes 737288 | tf_op jit(solution)/shard_map/ppermute | solution.py:21
  36.3 1.9 %collective-permute-start.4 = (f32[3,80,256]{2,1,0:T(8,128)S(1)}, f32[3,80,256]{2,1,0:T(8,128)S(1)}, u32[]{:S(2)}, u32[]{:S(2)}) collective-permute-start(f32[3,80,256]{2,1,0:T(8,128)S(1)} %multiply_add_fusion.2), channel_id=1, source_target_pairs={{0,1},{1,2},{2,3},{3,4},{4,5},{5,6},{6,7},{7,8},{8,9},{9,10},{10,1... | collective-permute-start | bytes 737288 | tf_op jit(solution)/shard_map/ppermute | solution.py:19
  38.2 3.2 %collective-permute-done.5 = f32[3,80,256]{2,1,0:T(8,128)S(1)} collective-permute-done((f32[3,80,256]{2,1,0:T(8,128)S(1)}, f32[3,80,256]{2,1,0:T(8,128)S(1)}, u32[]{:S(2)}, u32[]{:S(2)}) %collective-permute-start.5) | collective-permute-done | bytes 245792 | tf_op jit(solution)/shard_map/ppermute | solution.py:21
  41.4 9.3 %collective-permute-done.4 = f32[3,80,256]{2,1,0:T(8,128)S(1)} collective-permute-done((f32[3,80,256]{2,1,0:T(8,128)S(1)}, f32[3,80,256]{2,1,0:T(8,128)S(1)}, u32[]{:S(2)}, u32[]{:S(2)}) %collective-permute-start.4) | collective-permute-done | bytes 245792 | tf_op jit(solution)/shard_map/ppermute | solution.py:19
  50.7 3.2 %collective-permute-start.7 = (f32[9,3,256]{2,1,0:T(4,128)S(1)}, f32[9,3,256]{2,1,0:T(4,128)S(1)}, u32[]{:S(2)}, u32[]{:S(2)}) collective-permute-start(f32[9,3,256]{2,1,0:T(4,128)S(1)} %get-tuple-element.8), channel_id=1, source_target_pairs={{256,0},{0,256},{257,1},{1,257},{258,2},{2,258},{259,3},{3,259},{2... | collective-permute-start | bytes 82952 | tf_op jit(solution)/shard_map/ppermute | solution.py:21
  53.9 1.9 %collective-permute-start.6 = (f32[9,3,256]{2,1,0:T(4,128)S(1)}, f32[9,3,256]{2,1,0:T(4,128)S(1)}, u32[]{:S(2)}, u32[]{:S(2)}) collective-permute-start(f32[9,3,256]{2,1,0:T(4,128)S(1)} %get-tuple-element.7), channel_id=1, source_target_pairs={{0,256},{256,0},{1,257},{257,1},{2,258},{258,2},{3,259},{259,3},{4... | collective-permute-start | bytes 82952 | tf_op jit(solution)/shard_map/ppermute | solution.py:19
  55.9 0.1 pad_maximum_fusion.3
  55.9 0.1 slice_subtract_fusion.1
  56.0 0.0 collective-permute-done.7
  56.0 1.1 %collective-permute-done.6 = f32[9,3,256]{2,1,0:T(4,128)S(1)} collective-permute-done((f32[9,3,256]{2,1,0:T(4,128)S(1)}, f32[9,3,256]{2,1,0:T(4,128)S(1)}, u32[]{:S(2)}, u32[]{:S(2)}) %collective-permute-start.6) | collective-permute-done | bytes 27680 | tf_op jit(solution)/shard_map/ppermute | solution.py:19
  57.0 0.1 pad_maximum_fusion.1
  57.2 0.3 fusion.1
  57.4 3.6 %multiply_add_fusion.1 = f32[3,80,256]{2,1,0:T(8,128)S(1)} fusion(f32[3,80,256]{2,1,0:T(8,128)S(1)} %multiply_add_fusion.2, f32[3,85,256]{2,1,0:T(8,128)S(1)} %slice_subtract_fusion.4, f32[3,80,261]{2,1,0:T(8,128)S(1)} %fusion.1, f32[8,80,256]{2,1,0:T(8,128)S(1)} %slice_subtract_fusion.1, f32[3,80,256]{2,1,0:T(8,128)S(1)} %copy-done, ...), kind=kLoop, calls=%fused_computation.21 | loop fusion | flops 24453120 | bytes 5162244 | tf_op jit(solution)/shard_map/add | solution.py:111
  61.1 1.9 %collective-permute-start.9 = (f32[3,80,256]{2,1,0:T(8,128)S(1)}, f32[3,80,256]{2,1,0:T(8,128)S(1)}, u32[]{:S(2)}, u32[]{:S(2)}) collective-permute-start(f32[3,80,256]{2,1,0:T(8,128)S(1)} %multiply_add_fusion.1), channel_id=1, source_target_pairs={{1,0},{2,1},{3,2},{4,3},{5,4},{6,5},{7,6},{8,7},{9,8},{10,9},{11,1... | collective-permute-start | bytes 737288 | tf_op jit(solution)/shard_map/ppermute | solution.py:21
  63.0 3.4 %collective-permute-start.8 = (f32[3,80,256]{2,1,0:T(8,128)S(1)}, f32[3,80,256]{2,1,0:T(8,128)S(1)}, u32[]{:S(2)}, u32[]{:S(2)}) collective-permute-start(f32[3,80,256]{2,1,0:T(8,128)S(1)} %multiply_add_fusion.1), channel_id=1, source_target_pairs={{0,1},{1,2},{2,3},{3,4},{4,5},{5,6},{6,7},{7,8},{8,9},{9,10},{10,1... | collective-permute-start | bytes 737288 | tf_op jit(solution)/shard_map/ppermute | solution.py:19
  66.4 3.9 %collective-permute-done.9 = f32[3,80,256]{2,1,0:T(8,128)S(1)} collective-permute-done((f32[3,80,256]{2,1,0:T(8,128)S(1)}, f32[3,80,256]{2,1,0:T(8,128)S(1)}, u32[]{:S(2)}, u32[]{:S(2)}) %collective-permute-start.9) | collective-permute-done | bytes 245792 | tf_op jit(solution)/shard_map/ppermute | solution.py:21
  70.3 7.4 %collective-permute-done.8 = f32[3,80,256]{2,1,0:T(8,128)S(1)} collective-permute-done((f32[3,80,256]{2,1,0:T(8,128)S(1)}, f32[3,80,256]{2,1,0:T(8,128)S(1)}, u32[]{:S(2)}, u32[]{:S(2)}) %collective-permute-start.8) | collective-permute-done | bytes 245792 | tf_op jit(solution)/shard_map/ppermute | solution.py:19
  77.7 2.9 %collective-permute-start.11 = (f32[9,3,256]{2,1,0:T(4,128)S(1)}, f32[9,3,256]{2,1,0:T(4,128)S(1)}, u32[]{:S(2)}, u32[]{:S(2)}) collective-permute-start(f32[9,3,256]{2,1,0:T(4,128)S(1)} %get-tuple-element.6), channel_id=1, source_target_pairs={{256,0},{0,256},{257,1},{1,257},{258,2},{2,258},{259,3},{3,259},{2... | collective-permute-start | bytes 82952 | tf_op jit(solution)/shard_map/ppermute | solution.py:21
  80.6 1.9 %collective-permute-start.10 = (f32[9,3,256]{2,1,0:T(4,128)S(1)}, f32[9,3,256]{2,1,0:T(4,128)S(1)}, u32[]{:S(2)}, u32[]{:S(2)}) collective-permute-start(f32[9,3,256]{2,1,0:T(4,128)S(1)} %get-tuple-element.5), channel_id=1, source_target_pairs={{0,256},{256,0},{1,257},{257,1},{2,258},{258,2},{3,259},{259,3},{4... | collective-permute-start | bytes 82952 | tf_op jit(solution)/shard_map/ppermute | solution.py:19
  82.6 0.1 pad_maximum_fusion.4
  82.6 0.1 slice_subtract_fusion
  82.7 0.0 collective-permute-done.11
  82.7 1.1 %collective-permute-done.10 = f32[9,3,256]{2,1,0:T(4,128)S(1)} collective-permute-done((f32[9,3,256]{2,1,0:T(4,128)S(1)}, f32[9,3,256]{2,1,0:T(4,128)S(1)}, u32[]{:S(2)}, u32[]{:S(2)}) %collective-permute-start.10) | collective-permute-done | bytes 27680 | tf_op jit(solution)/shard_map/ppermute | solution.py:19
  83.7 0.1 pad_maximum_fusion.2
  83.9 0.3 fusion.2
  84.1 4.3 %multiply_add_fusion = f32[3,80,256]{2,1,0:T(8,128)} fusion(f32[3,80,256]{2,1,0:T(8,128)S(1)} %multiply_add_fusion.1, f32[3,85,256]{2,1,0:T(8,128)S(1)} %slice_subtract_fusion.3, f32[3,80,261]{2,1,0:T(8,128)S(1)} %fusion.2, f32[8,80,256]{2,1,0:T(8,128)S(1)} %slice_subtract_fusion, f32[3,80,256]{2,1,0:T(8,128)S(1)} %copy-done, f32[80]{0:T(128)S(1)} %get-tuple-element.11, ...), kind=kLoop, calls=%fused_computation.20 | loop fusion | flops 24453120 | bytes 5162244 | tf_op jit(solution)/shard_map/add | solution.py:112
  (10 shorter events, 0.3 us)
Async XLA Ops:
  0.0 14.4 %collective-permute-start = (f32[3,80,256]{2,1,0:T(8,128)}, f32[3,80,256]{2,1,0:T(8,128)S(1)}, u32[]{:S(2)}, u32[]{:S(2)}) collective-permute-start(f32[3,80,256]{2,1,0:T(8,128)} %param.2), channel_id=1, source_target_pairs={{0,1},{1,2},{2,3},{3,4},{4,5},{5,6},{6,7},{7,8},{8,9},{9,10},{10,1... | collective-permute-start | bytes 737288 | tf_op jit(solution)/shard_map/ppermute | solution.py:19
  3.1 12.3 %collective-permute-start.1 = (f32[3,80,256]{2,1,0:T(8,128)}, f32[3,80,256]{2,1,0:T(8,128)S(1)}, u32[]{:S(2)}, u32[]{:S(2)}) collective-permute-start(f32[3,80,256]{2,1,0:T(8,128)} %param.2), channel_id=1, source_target_pairs={{1,0},{2,1},{3,2},{4,3},{5,4},{6,5},{7,6},{8,7},{9,8},{10,9},{11,1... | collective-permute-start | bytes 737288 | tf_op jit(solution)/shard_map/ppermute | solution.py:21
  15.4 5.7 %collective-permute-start.3 = (f32[9,3,256]{2,1,0:T(4,128)S(1)}, f32[9,3,256]{2,1,0:T(4,128)S(1)}, u32[]{:S(2)}, u32[]{:S(2)}) collective-permute-start(f32[9,3,256]{2,1,0:T(4,128)S(1)} %get-tuple-element.10), channel_id=1, source_target_pairs={{256,0},{0,256},{257,1},{1,257},{258,2},{2,258},{259,3},{3,259},{2... | collective-permute-start | bytes 82952 | tf_op jit(solution)/shard_map/ppermute | solution.py:21
  19.1 3.1 %collective-permute-start.2 = (f32[9,3,256]{2,1,0:T(4,128)S(1)}, f32[9,3,256]{2,1,0:T(4,128)S(1)}, u32[]{:S(2)}, u32[]{:S(2)}) collective-permute-start(f32[9,3,256]{2,1,0:T(4,128)S(1)} %get-tuple-element.9), channel_id=1, source_target_pairs={{0,256},{256,0},{1,257},{257,1},{2,258},{258,2},{3,259},{259,3},{4... | collective-permute-start | bytes 82952 | tf_op jit(solution)/shard_map/ppermute | solution.py:19
  22.3 0.9 %copy-start = (f32[3,80,256]{2,1,0:T(8,128)S(1)}, f32[3,80,256]{2,1,0:T(8,128)}, u32[]{:S(2)}) copy-start(f32[3,80,256]{2,1,0:T(8,128)} %param.2) | copy-start | bytes 737284
  26.9 14.6 %collective-permute-start.5 = (f32[3,80,256]{2,1,0:T(8,128)S(1)}, f32[3,80,256]{2,1,0:T(8,128)S(1)}, u32[]{:S(2)}, u32[]{:S(2)}) collective-permute-start(f32[3,80,256]{2,1,0:T(8,128)S(1)} %multiply_add_fusion.2), channel_id=1, source_target_pairs={{1,0},{2,1},{3,2},{4,3},{5,4},{6,5},{7,6},{8,7},{9,8},{10,9},{11,1... | collective-permute-start | bytes 737288 | tf_op jit(solution)/shard_map/ppermute | solution.py:21
  36.3 14.4 %collective-permute-start.4 = (f32[3,80,256]{2,1,0:T(8,128)S(1)}, f32[3,80,256]{2,1,0:T(8,128)S(1)}, u32[]{:S(2)}, u32[]{:S(2)}) collective-permute-start(f32[3,80,256]{2,1,0:T(8,128)S(1)} %multiply_add_fusion.2), channel_id=1, source_target_pairs={{0,1},{1,2},{2,3},{3,4},{4,5},{5,6},{6,7},{7,8},{8,9},{9,10},{10,1... | collective-permute-start | bytes 737288 | tf_op jit(solution)/shard_map/ppermute | solution.py:19
  50.7 5.3 %collective-permute-start.7 = (f32[9,3,256]{2,1,0:T(4,128)S(1)}, f32[9,3,256]{2,1,0:T(4,128)S(1)}, u32[]{:S(2)}, u32[]{:S(2)}) collective-permute-start(f32[9,3,256]{2,1,0:T(4,128)S(1)} %get-tuple-element.8), channel_id=1, source_target_pairs={{256,0},{0,256},{257,1},{1,257},{258,2},{2,258},{259,3},{3,259},{2... | collective-permute-start | bytes 82952 | tf_op jit(solution)/shard_map/ppermute | solution.py:21
  53.9 3.1 %collective-permute-start.6 = (f32[9,3,256]{2,1,0:T(4,128)S(1)}, f32[9,3,256]{2,1,0:T(4,128)S(1)}, u32[]{:S(2)}, u32[]{:S(2)}) collective-permute-start(f32[9,3,256]{2,1,0:T(4,128)S(1)} %get-tuple-element.7), channel_id=1, source_target_pairs={{0,256},{256,0},{1,257},{257,1},{2,258},{258,2},{3,259},{259,3},{4... | collective-permute-start | bytes 82952 | tf_op jit(solution)/shard_map/ppermute | solution.py:19
  61.1 9.2 %collective-permute-start.9 = (f32[3,80,256]{2,1,0:T(8,128)S(1)}, f32[3,80,256]{2,1,0:T(8,128)S(1)}, u32[]{:S(2)}, u32[]{:S(2)}) collective-permute-start(f32[3,80,256]{2,1,0:T(8,128)S(1)} %multiply_add_fusion.1), channel_id=1, source_target_pairs={{1,0},{2,1},{3,2},{4,3},{5,4},{6,5},{7,6},{8,7},{9,8},{10,9},{11,1... | collective-permute-start | bytes 737288 | tf_op jit(solution)/shard_map/ppermute | solution.py:21
  63.0 14.7 %collective-permute-start.8 = (f32[3,80,256]{2,1,0:T(8,128)S(1)}, f32[3,80,256]{2,1,0:T(8,128)S(1)}, u32[]{:S(2)}, u32[]{:S(2)}) collective-permute-start(f32[3,80,256]{2,1,0:T(8,128)S(1)} %multiply_add_fusion.1), channel_id=1, source_target_pairs={{0,1},{1,2},{2,3},{3,4},{4,5},{5,6},{6,7},{7,8},{8,9},{9,10},{10,1... | collective-permute-start | bytes 737288 | tf_op jit(solution)/shard_map/ppermute | solution.py:19
  77.7 5.0 %collective-permute-start.11 = (f32[9,3,256]{2,1,0:T(4,128)S(1)}, f32[9,3,256]{2,1,0:T(4,128)S(1)}, u32[]{:S(2)}, u32[]{:S(2)}) collective-permute-start(f32[9,3,256]{2,1,0:T(4,128)S(1)} %get-tuple-element.6), channel_id=1, source_target_pairs={{256,0},{0,256},{257,1},{1,257},{258,2},{2,258},{259,3},{3,259},{2... | collective-permute-start | bytes 82952 | tf_op jit(solution)/shard_map/ppermute | solution.py:21
  80.6 3.1 %collective-permute-start.10 = (f32[9,3,256]{2,1,0:T(4,128)S(1)}, f32[9,3,256]{2,1,0:T(4,128)S(1)}, u32[]{:S(2)}, u32[]{:S(2)}) collective-permute-start(f32[9,3,256]{2,1,0:T(4,128)S(1)} %get-tuple-element.5), channel_id=1, source_target_pairs={{0,256},{256,0},{1,257},{257,1},{2,258},{258,2},{3,259},{259,3},{4... | collective-permute-start | bytes 82952 | tf_op jit(solution)/shard_map/ppermute | solution.py:19
where the time goes:
time: 88.8 us; the launch traced here: 88.4 us
  starting transfers between devices  43 us (48%)
  waiting for transfers between devices  29.9 us (34%)
  other arithmetic  12.9 us (15%)
  local copies, waits for them, and re-layouts  1.65 us (2%)
  between operations  0.94 us (1%)
    ppermute x6, starting transfers between devices, extended_2(): lax.ppermute(head, axis, [((i + 1) % count, i) for i in range(ends)])  28.8 us
    ppermute x6, waiting for transfers between devices, extended_2(): lax.ppermute(tail, axis, [(i, (i + 1) % count) for i in range(ends)])  22.7 us
    ppermute x6, starting transfers between devices, extended_2(): lax.ppermute(tail, axis, [(i, (i + 1) % count) for i in range(ends)])  14.2 us
    ppermute x6, waiting for transfers between devices, extended_2(): lax.ppermute(head, axis, [((i + 1) % count, i) for i in range(ends)])  7.17 us
    add x1, other arithmetic, on_device(): level_set / 3.0  4.25 us
    add x1, other arithmetic, on_device(): 0.75 * level_set  3.63 us
    add x1, other arithmetic, on_device(): section_one = level_set + step_size * section_rate(level_set)  3.57 us
  transfers between devices with their start and end apart: 12, of which 8 were waited for; matrix products, arithmetic and copies ran while one was open for 1% of the time, Pallas kernels for 0%

commit v1 on v0

v1 whole, which is shorter than its diff:
```python
import jax
import jax.numpy as jnp
from jax import lax
from jax.sharding import PartitionSpec as P


def weno_pair(d0, d1, d2, d3, d4, d5):
    e0, e1, e2, e3, e4 = d1 - d0, d2 - d1, d3 - d2, d4 - d3, d5 - d4

    def base(e, f):
        t = f - e
        return (13.0 / 3.0) * (t * t) + 4e-6

    def sq(v):
        return v * v

    t0, t1, t2, t3 = base(e0, e1), base(e1, e2), base(e2, e3), base(e3, e4)
    a0 = t0 + sq(3.0 * e1 - e0)
    a1 = t1 + sq(3.0 * e2 - e1)
    b1 = t1 + sq(e1 + e2)
    b2 = t2 + sq(e2 + e3)
    c2 = t2 + sq(3.0 * e2 - e3)
    c3 = t3 + sq(3.0 * e3 - e4)

    def side(s1, s2, s3, q1, q2, q3):
        w1, w2, w3 = sq(s2 * s3), 6.0 * sq(s1 * s3), 3.0 * sq(s1 * s2)
        return (w1 * q1 + w2 * q2 + w3 * q3) / (6.0 * (w1 + w2 + w3))

    minus = d2 + side(a0, b1, c2, 5.0 * e1 - 2.0 * e0, e1 + 2.0 * e2, 4.0 * e2 - e3)
    plus = d3 - side(c3, b2, a1, 5.0 * e3 - 2.0 * e4, e3 + 2.0 * e2, 4.0 * e2 - e1)
    return minus, plus


def one_sided(padded, axis, count):
    d = lax.slice_in_dim(padded, 1, count + 6, axis=axis) - lax.slice_in_dim(padded, 0, count + 5, axis=axis)
    return weno_pair(*[lax.slice_in_dim(d, k, k + count, axis=axis) for k in range(6)])


def on_device(level_set, step_length):
    step = step_length[0]
    rows_x, rows_h, _ = level_set.shape
    count = lax.axis_size("ha")
    even = [p for j in range(0, count - 1, 2) for p in ((j, j + 1), (j + 1, j))]
    odd = [p for j in range(1, count - 1, 2) for p in ((j, j + 1), (j + 1, j))]
    is_odd = lax.axis_index("ha") % 2 == 1
    total_h = lax.axis_size("gx") * rows_h
    global_h = lax.axis_index("gx") * rows_h + jnp.arange(rows_h, dtype=jnp.int32)
    heading = 2.0 * jnp.pi * global_h.astype(jnp.float32) / total_h
    cos_grid = jnp.cos(heading)[None, :, None]
    sin_grid = jnp.sin(heading)[None, :, None]

    def rate(u):
        from_odd = lax.ppermute(u, "ha", odd)
        from_even = lax.ppermute(u, "ha", even)
        edges = jnp.concatenate([u[:, :3], u[:, -3:]], axis=1)
        edges = lax.ppermute(edges, "gx", [(0, 1), (1, 0)])
        minus_y, plus_y = one_sided(jnp.pad(u, ((0, 0), (0, 0), (3, 3))), 2, u.shape[2])
        minus_h, plus_h = one_sided(jnp.concatenate([edges[:, 3:], u, edges[:, :3]], axis=1), 1, rows_h)
        ham = 0.5 * (sin_grid * (minus_y + plus_y) - jnp.abs(minus_h + plus_h))
        damp = 0.5 * (jnp.abs(sin_grid) * (plus_y - minus_y) + (plus_h - minus_h))
        ham, damp = lax.optimization_barrier((ham, damp))
        left = jnp.where(is_odd, from_even, from_odd)
        right = jnp.where(is_odd, from_odd, from_even)
        minus_x, plus_x = one_sided(jnp.concatenate([left, u, right], axis=0), 0, rows_x)
        ham = ham + (0.5 * cos_grid) * (minus_x + plus_x)
        damp = damp + (0.5 * jnp.abs(cos_grid)) * (plus_x - minus_x)
        return damp - jnp.maximum(0.0, -ham)

    one = level_set + step * rate(level_set)
    two = 0.75 * level_set + 0.25 * (one + step * rate(one))
    return level_set / 3.0 + 2.0 / 3.0 * (two + step * rate(two))


def solution(mesh):
    return jax.shard_map(
        on_device,
        mesh=mesh,
        in_specs=(P("ha", "gx", None), P()),
        out_specs=P("ha", "gx", None),
        check_vma=False,
    )
```

time: 88.8 us -> 61.7 us (0.69)
  waiting for transfers between devices: 29.9 us -> 14.7 us
  starting transfers between devices: 43 us -> 33.8 us
  other arithmetic: 12.9 us -> 10.8 us
    ppermute x12 -> x9, waiting for transfers between devices: 29.9 us -> 14.7 us  [the longest x3 14.7 us: rate(): from_odd = lax.ppermute(u, 'ha', odd)]
    ppermute x12 -> x9, starting transfers between devices: 43 us -> 33.8 us  [the longest x3 17.2 us: rate(): from_odd = lax.ppermute(u, 'ha', odd)]
    add x3, other arithmetic: 11.5 us -> 2.78 us  [the longest x1 1.4 us: on_device(): return level_set / 3.0 + 2.0 / 3.0 * (two + step * rate(two))]
    mul x0 -> x8, other arithmetic: none -> 5.48 us  [the longest x3 5.08 us: rate(): damp = 0.5 * (jnp.abs(sin_grid) * (plus_y - minus_y) + (plus_h - minus_h))]
    unnamed x4 -> x2, local copies, waits for them, and re-layouts: 1.62 us -> 0.01 us
    sub x9, other arithmetic: 1.01 us -> 2.12 us  [one_sided(): lax.slice_in_dim(padded, 1, count + 6, axis=axis)]
  transfers between devices with their start and end apart: 12 -> 9, of which waited for: 8 -> 3; matrix products, arithmetic and copies ran while one was open for 1% -> 14% of each run, Pallas kernels for 0% -> 0%
where the time goes in v1:
time: 61.7 us; the launch traced here: 61.1 us
  starting transfers between devices  33.8 us (55%)
  waiting for transfers between devices  14.7 us (24%)
  other arithmetic  10.8 us (18%)
  between operations  1.02 us (2%)
  local copies, waits for them, and re-layouts  0.83 us (1%)
    ppermute x3, starting transfers between devices, rate(): from_odd = lax.ppermute(u, 'ha', odd)  17.2 us
    ppermute x3, waiting for transfers between devices, rate(): from_odd = lax.ppermute(u, 'ha', odd)  14.7 us
    ppermute x3, starting transfers between devices, rate(): edges = lax.ppermute(edges, 'gx', [(0, 1), (1, 0)])  9.64 us
    ppermute x3, starting transfers between devices, rate(): from_even = lax.ppermute(u, 'ha', even)  6.95 us
    mul x3, other arithmetic, rate(): damp = 0.5 * (jnp.abs(sin_grid) * (plus_y - minus_y) + (plus_h - minus_h))  5.08 us
    sub x9, other arithmetic, one_sided(): lax.slice_in_dim(padded, 1, count + 6, axis=axis)  2.12 us
    add x1, other arithmetic, on_device(): return level_set / 3.0 + 2.0 / 3.0 * (two + step * rate(two))  1.4 us
  transfers between devices with their start and end apart: 9, of which 3 were waited for; matrix products, arithmetic and copies ran while one was open for 14% of the time, Pallas kernels for 0%

profile of v1, /device:TPU:257, one launch (start us, length us, event | category | flops | bytes accessed | tf_op | source)
XLA Modules:
  0.0 61.1 jit_solution(5554989745848557501)
XLA Ops:
  0.0 3.1 %collective-permute-start.1 = (f32[3,80,256]{2,1,0:T(8,128)}, f32[3,80,256]{2,1,0:T(8,128)S(1)}, u32[]{:S(2)}, u32[]{:S(2)}) collective-permute-start(f32[3,80,256]{2,1,0:T(8,128)} %param.2), channel_id=1, source_target_pairs={{0,1},{1,0},{2,3},{3,2},{4,5},{5,4},{6,7},{7,6},{8,9},{9,8},{10,11... | collective-permute-start | bytes 737288 | tf_op jit(solution)/shard_map/ppermute | solution.py:54
  3.1 5.7 %collective-permute-start.2 = (f32[3,80,256]{2,1,0:T(8,128)}, f32[3,80,256]{2,1,0:T(8,128)S(1)}, u32[]{:S(2)}, u32[]{:S(2)}) collective-permute-start(f32[3,80,256]{2,1,0:T(8,128)} %param.2), channel_id=1, source_target_pairs={{1,2},{2,1},{3,4},{4,3},{5,6},{6,5},{7,8},{8,7},{9,10},{10,9},{11,... | collective-permute-start | bytes 737288 | tf_op jit(solution)/shard_map/ppermute | solution.py:53
  8.8 0.8 %fusion.26 = (f32[3,3,256]{2,1,0:T(4,128)S(1)}, f32[3,3,256]{2,1,0:T(4,128)S(1)}) fusion(f32[3,80,256]{2,1,0:T(8,128)} %param.2), kind=kLoop, calls=%fused_computation.125 | loop fusion | bytes 36864 | tf_op jit(solution)/shard_map/slice | solution.py:55
  9.7 3.1 %collective-permute-start = (f32[3,6,256]{2,1,0:T(8,128)S(1)}, f32[3,6,256]{2,1,0:T(8,128)S(1)}, u32[]{:S(2)}, u32[]{:S(2)}) collective-permute-start(f32[3,6,256]{2,1,0:T(8,128)S(1)} %pad_maximum_fusion.6), channel_id=1, source_target_pairs={{0,256},{256,0},{1,257},{257,1},{2,258},{258,2},{3,259},{259,3},{4... | collective-permute-start | bytes 55304 | tf_op jit(solution)/shard_map/ppermute | solution.py:56
  12.8 0.0 copy-start
  12.8 1.4 %fusion = f32[3,80,261]{2,1,0:T(8,128)S(1)} fusion(f32[3,80,256]{2,1,0:T(8,128)} %param.2), kind=kLoop, calls=%fused_computation.12 | loop fusion | flops 62640 | bytes 496320 | tf_op jit(solution)/shard_map/sub | solution.py:35
  14.9 0.0 collective-permute-done
  15.0 0.0 copy-done
  15.1 1.7 %add_multiply_fusion.2 = (f32[3,80,256]{2,1,0:T(8,128)S(1)}, f32[3,80,256]{2,1,0:T(8,128)S(1)}, f32[3,80,256]{2,1,0:T(8,128)S(1)}, f32[3,80,256]{2,1,0:T(8,128)S(1)}, f32[3,80,256]{2,1,0:T(8,128)S(1)}) fusion(f32[80]{0:T(128)S(1)} %get-tuple-element.53, f32[3,80,261]{2,1,0:T(8,128)S(1)} %fusion, f32[3,85,256]{2,1,0:T(8,128)S(1)} %slice_subtract_fusion.5), kind=kLoop, calls=%fused_computation.86 | loop fusion | flops 11366400 | bytes 4178240 | tf_op jit(solution)/shard_map/mul | solution.py:60
  16.8 0.1 subtract_multiply_fusion.2
  16.9 0.0 collective-permute-done.1
  16.9 0.3 collective-permute-done.2
  17.3 0.1 pad_maximum_fusion
  17.3 0.1 slice_subtract_fusion.2
  17.4 0.7 %multiply_add_fusion.10 = f32[3,80,256]{2,1,0:T(8,128)S(1)} fusion(f32[3,80,256]{2,1,0:T(8,128)S(1)} %copy-done, f32[3,80,256]{2,1,0:T(8,128)S(1)} %subtract_multiply_fusion.2, f32[3,80,256]{2,1,0:T(8,128)S(1)} %get-tuple-element.11, f32[8,80,256]{2,1,0:T(8,128)S(1)} %slice_subtract_fusion.2, f32[80]{0:T(128)S(1)} %get-tuple-element.52, ...), kind=kLoop, calls=%fused_computation.77 | loop fusion | flops 6205440 | bytes 2458244 | tf_op jit(solution)/shard_map/add | solution.py:69
  18.1 3.7 %collective-permute-start.3 = (f32[3,6,256]{2,1,0:T(8,128)S(1)}, f32[3,6,256]{2,1,0:T(8,128)S(1)}, u32[]{:S(2)}, u32[]{:S(2)}) collective-permute-start(f32[3,6,256]{2,1,0:T(8,128)S(1)} %pad_maximum_fusion.7), channel_id=1, source_target_pairs={{0,256},{256,0},{1,257},{257,1},{2,258},{258,2},{3,259},{259,3},{4... | collective-permute-start | bytes 55304 | tf_op jit(solution)/shard_map/ppermute | solution.py:56
  21.8 0.3 fusion.1
  22.1 1.9 %collective-permute-start.4 = (f32[3,80,256]{2,1,0:T(8,128)S(1)}, f32[3,80,256]{2,1,0:T(8,128)S(1)}, u32[]{:S(2)}, u32[]{:S(2)}) collective-permute-start(f32[3,80,256]{2,1,0:T(8,128)S(1)} %multiply_add_fusion.10), channel_id=1, source_target_pairs={{0,1},{1,0},{2,3},{3,2},{4,5},{5,4},{6,7},{7,6},{8,9},{9,8},{10,11... | collective-permute-start | bytes 737288 | tf_op jit(solution)/shard_map/ppermute | solution.py:54
  24.0 5.7 %collective-permute-start.5 = (f32[3,80,256]{2,1,0:T(8,128)S(1)}, f32[3,80,256]{2,1,0:T(8,128)S(1)}, u32[]{:S(2)}, u32[]{:S(2)}) collective-permute-start(f32[3,80,256]{2,1,0:T(8,128)S(1)} %multiply_add_fusion.10), channel_id=1, source_target_pairs={{1,2},{2,1},{3,4},{4,3},{5,6},{6,5},{7,8},{8,7},{9,10},{10,9},{11,... | collective-permute-start | bytes 737288 | tf_op jit(solution)/shard_map/ppermute | solution.py:53
  29.7 0.0 collective-permute-done.3
  29.8 1.7 %add_multiply_fusion.1 = (f32[3,80,256]{2,1,0:T(8,128)S(1)}, f32[3,80,256]{2,1,0:T(8,128)S(1)}, f32[3,80,256]{2,1,0:T(8,128)S(1)}, f32[3,80,256]{2,1,0:T(8,128)S(1)}, f32[3,80,256]{2,1,0:T(8,128)S(1)}) fusion(f32[80]{0:T(128)S(1)} %get-tuple-element.53, f32[3,80,261]{2,1,0:T(8,128)S(1)} %fusion.1, f32[3,85,256]{2,1,0:T(8,128)S(1)} %slice_subtract_fusion.4), kind=kLoop, calls=%fused_computation.67 | loop fusion | flops 11366400 | bytes 4178240 | tf_op jit(solution)/shard_map/mul | solution.py:60
  31.5 0.1 subtract_multiply_fusion.1
  31.6 0.0 collective-permute-done.4
  31.6 7.2 %collective-permute-done.5 = f32[3,80,256]{2,1,0:T(8,128)S(1)} collective-permute-done((f32[3,80,256]{2,1,0:T(8,128)S(1)}, f32[3,80,256]{2,1,0:T(8,128)S(1)}, u32[]{:S(2)}, u32[]{:S(2)}) %collective-permute-start.5) | collective-permute-done | bytes 245792 | tf_op jit(solution)/shard_map/ppermute | solution.py:53
  38.9 0.1 pad_maximum_fusion.1
  38.9 0.1 slice_subtract_fusion.1
  39.0 0.7 %multiply_add_fusion.5 = f32[3,80,256]{2,1,0:T(8,128)S(1)} fusion(f32[3,80,256]{2,1,0:T(8,128)S(1)} %multiply_add_fusion.10, f32[3,80,256]{2,1,0:T(8,128)S(1)} %subtract_multiply_fusion.1, f32[3,80,256]{2,1,0:T(8,128)S(1)} %get-tuple-element.13, f32[8,80,256]{2,1,0:T(8,128)S(1)} %slice_subtract_fusion.1, f32[3,80,256]{2,1,0:T(8,128)S(1)} %copy-done, ...), kind=kLoop, calls=%fused_computation.58 | loop fusion | flops 6389760 | bytes 2704004 | tf_op jit(solution)/shard_map/add | solution.py:70
  39.7 2.8 %collective-permute-start.6 = (f32[3,6,256]{2,1,0:T(8,128)S(1)}, f32[3,6,256]{2,1,0:T(8,128)S(1)}, u32[]{:S(2)}, u32[]{:S(2)}) collective-permute-start(f32[3,6,256]{2,1,0:T(8,128)S(1)} %pad_maximum_fusion.8), channel_id=1, source_target_pairs={{0,256},{256,0},{1,257},{257,1},{2,258},{258,2},{3,259},{259,3},{4... | collective-permute-start | bytes 55304 | tf_op jit(solution)/shard_map/ppermute | solution.py:56
  42.5 0.3 fusion.2
  42.8 1.9 %collective-permute-start.7 = (f32[3,80,256]{2,1,0:T(8,128)S(1)}, f32[3,80,256]{2,1,0:T(8,128)S(1)}, u32[]{:S(2)}, u32[]{:S(2)}) collective-permute-start(f32[3,80,256]{2,1,0:T(8,128)S(1)} %multiply_add_fusion.5), channel_id=1, source_target_pairs={{0,1},{1,0},{2,3},{3,2},{4,5},{5,4},{6,7},{7,6},{8,9},{9,8},{10,11... | collective-permute-start | bytes 737288 | tf_op jit(solution)/shard_map/ppermute | solution.py:54
  44.7 5.7 %collective-permute-start.8 = (f32[3,80,256]{2,1,0:T(8,128)S(1)}, f32[3,80,256]{2,1,0:T(8,128)S(1)}, u32[]{:S(2)}, u32[]{:S(2)}) collective-permute-start(f32[3,80,256]{2,1,0:T(8,128)S(1)} %multiply_add_fusion.5), channel_id=1, source_target_pairs={{1,2},{2,1},{3,4},{4,3},{5,6},{6,5},{7,8},{8,7},{9,10},{10,9},{11,... | collective-permute-start | bytes 737288 | tf_op jit(solution)/shard_map/ppermute | solution.py:53
  50.4 0.0 collective-permute-done.6
  50.5 1.7 %add_multiply_fusion = (f32[3,80,256]{2,1,0:T(8,128)S(1)}, f32[3,80,256]{2,1,0:T(8,128)S(1)}, f32[3,80,256]{2,1,0:T(8,128)S(1)}, f32[3,80,256]{2,1,0:T(8,128)S(1)}, f32[3,80,256]{2,1,0:T(8,128)S(1)}) fusion(f32[80]{0:T(128)S(1)} %get-tuple-element.53, f32[3,80,261]{2,1,0:T(8,128)S(1)} %fusion.2, f32[3,85,256]{2,1,0:T(8,128)S(1)} %slice_subtract_fusion.3), kind=kLoop, calls=%fused_computation.48 | loop fusion | flops 11366400 | bytes 4178240 | tf_op jit(solution)/shard_map/mul | solution.py:60
  52.2 0.1 subtract_multiply_fusion
  52.3 0.0 collective-permute-done.7
  52.3 7.2 %collective-permute-done.8 = f32[3,80,256]{2,1,0:T(8,128)S(1)} collective-permute-done((f32[3,80,256]{2,1,0:T(8,128)S(1)}, f32[3,80,256]{2,1,0:T(8,128)S(1)}, u32[]{:S(2)}, u32[]{:S(2)}) %collective-permute-start.8) | collective-permute-done | bytes 245792 | tf_op jit(solution)/shard_map/ppermute | solution.py:53
  59.6 0.1 pad_maximum_fusion.2
  59.6 0.1 slice_subtract_fusion
  59.7 1.4 %multiply_add_fusion = f32[3,80,256]{2,1,0:T(8,128)} fusion(f32[3,80,256]{2,1,0:T(8,128)S(1)} %multiply_add_fusion.5, f32[3,80,256]{2,1,0:T(8,128)S(1)} %subtract_multiply_fusion, f32[3,80,256]{2,1,0:T(8,128)S(1)} %get-tuple-element.15, f32[8,80,256]{2,1,0:T(8,128)S(1)} %slice_subtract_fusion, f32[3,80,256]{2,1,0:T(8,128)S(1)} %copy-done, ...), kind=kLoop, calls=%fused_computation.39 | loop fusion | flops 6389760 | bytes 2704004 | tf_op jit(solution)/shard_map/add | solution.py:71
  (19 shorter events, 0.5 us)
Async XLA Ops:
  0.0 16.9 %collective-permute-start.1 = (f32[3,80,256]{2,1,0:T(8,128)}, f32[3,80,256]{2,1,0:T(8,128)S(1)}, u32[]{:S(2)}, u32[]{:S(2)}) collective-permute-start(f32[3,80,256]{2,1,0:T(8,128)} %param.2), channel_id=1, source_target_pairs={{0,1},{1,0},{2,3},{3,2},{4,5},{5,4},{6,7},{7,6},{8,9},{9,8},{10,11... | collective-permute-start | bytes 737288 | tf_op jit(solution)/shard_map/ppermute | solution.py:54
  3.1 14.1 %collective-permute-start.2 = (f32[3,80,256]{2,1,0:T(8,128)}, f32[3,80,256]{2,1,0:T(8,128)S(1)}, u32[]{:S(2)}, u32[]{:S(2)}) collective-permute-start(f32[3,80,256]{2,1,0:T(8,128)} %param.2), channel_id=1, source_target_pairs={{1,2},{2,1},{3,4},{4,3},{5,6},{6,5},{7,8},{8,7},{9,10},{10,9},{11,... | collective-permute-start | bytes 737288 | tf_op jit(solution)/shard_map/ppermute | solution.py:53
  9.7 5.3 %collective-permute-start = (f32[3,6,256]{2,1,0:T(8,128)S(1)}, f32[3,6,256]{2,1,0:T(8,128)S(1)}, u32[]{:S(2)}, u32[]{:S(2)}) collective-permute-start(f32[3,6,256]{2,1,0:T(8,128)S(1)} %pad_maximum_fusion.6), channel_id=1, source_target_pairs={{0,256},{256,0},{1,257},{257,1},{2,258},{258,2},{3,259},{259,3},{4... | collective-permute-start | bytes 55304 | tf_op jit(solution)/shard_map/ppermute | solution.py:56
  12.8 2.2 %copy-start = (f32[3,80,256]{2,1,0:T(8,128)S(1)}, f32[3,80,256]{2,1,0:T(8,128)}, u32[]{:S(2)}) copy-start(f32[3,80,256]{2,1,0:T(8,128)} %param.2) | copy-start | bytes 737284
  18.1 11.6 %collective-permute-start.3 = (f32[3,6,256]{2,1,0:T(8,128)S(1)}, f32[3,6,256]{2,1,0:T(8,128)S(1)}, u32[]{:S(2)}, u32[]{:S(2)}) collective-permute-start(f32[3,6,256]{2,1,0:T(8,128)S(1)} %pad_maximum_fusion.7), channel_id=1, source_target_pairs={{0,256},{256,0},{1,257},{257,1},{2,258},{258,2},{3,259},{259,3},{4... | collective-permute-start | bytes 55304 | tf_op jit(solution)/shard_map/ppermute | solution.py:56
  22.1 9.6 %collective-permute-start.4 = (f32[3,80,256]{2,1,0:T(8,128)S(1)}, f32[3,80,256]{2,1,0:T(8,128)S(1)}, u32[]{:S(2)}, u32[]{:S(2)}) collective-permute-start(f32[3,80,256]{2,1,0:T(8,128)S(1)} %multiply_add_fusion.10), channel_id=1, source_target_pairs={{0,1},{1,0},{2,3},{3,2},{4,5},{5,4},{6,7},{7,6},{8,9},{9,8},{10,11... | collective-permute-start | bytes 737288 | tf_op jit(solution)/shard_map/ppermute | solution.py:54
  24.0 14.8 %collective-permute-start.5 = (f32[3,80,256]{2,1,0:T(8,128)S(1)}, f32[3,80,256]{2,1,0:T(8,128)S(1)}, u32[]{:S(2)}, u32[]{:S(2)}) collective-permute-start(f32[3,80,256]{2,1,0:T(8,128)S(1)} %multiply_add_fusion.10), channel_id=1, source_target_pairs={{1,2},{2,1},{3,4},{4,3},{5,6},{6,5},{7,8},{8,7},{9,10},{10,9},{11,... | collective-permute-start | bytes 737288 | tf_op jit(solution)/shard_map/ppermute | solution.py:53
  39.7 10.7 %collective-permute-start.6 = (f32[3,6,256]{2,1,0:T(8,128)S(1)}, f32[3,6,256]{2,1,0:T(8,128)S(1)}, u32[]{:S(2)}, u32[]{:S(2)}) collective-permute-start(f32[3,6,256]{2,1,0:T(8,128)S(1)} %pad_maximum_fusion.8), channel_id=1, source_target_pairs={{0,256},{256,0},{1,257},{257,1},{2,258},{258,2},{3,259},{259,3},{4... | collective-permute-start | bytes 55304 | tf_op jit(solution)/shard_map/ppermute | solution.py:56
  42.8 9.6 %collective-permute-start.7 = (f32[3,80,256]{2,1,0:T(8,128)S(1)}, f32[3,80,256]{2,1,0:T(8,128)S(1)}, u32[]{:S(2)}, u32[]{:S(2)}) collective-permute-start(f32[3,80,256]{2,1,0:T(8,128)S(1)} %multiply_add_fusion.5), channel_id=1, source_target_pairs={{0,1},{1,0},{2,3},{3,2},{4,5},{5,4},{6,7},{7,6},{8,9},{9,8},{10,11... | collective-permute-start | bytes 737288 | tf_op jit(solution)/shard_map/ppermute | solution.py:54
  44.7 14.8 %collective-permute-start.8 = (f32[3,80,256]{2,1,0:T(8,128)S(1)}, f32[3,80,256]{2,1,0:T(8,128)S(1)}, u32[]{:S(2)}, u32[]{:S(2)}) collective-permute-start(f32[3,80,256]{2,1,0:T(8,128)S(1)} %multiply_add_fusion.5), channel_id=1, source_target_pairs={{1,2},{2,1},{3,4},{4,3},{5,6},{6,5},{7,8},{8,7},{9,10},{10,9},{11,... | collective-permute-start | bytes 737288 | tf_op jit(solution)/shard_map/ppermute | solution.py:53

commit v2 on v1

v2 whole, which is shorter than its diff:
```python
import functools

import jax
import jax.numpy as jnp
from jax import lax
from jax.experimental import pallas as pl
from jax.experimental.pallas import tpu as pltpu
from jax.sharding import PartitionSpec as P


def sq(c):
    return c * c


def corrections(e, t, s):
    base = [(13.0 / 3.0) * sq(c) + 4e-6 for c in t]
    triple = [3.0 * c for c in e]
    low = [sq(b + sq(triple[k + 1] - e[k])) for k, b in enumerate(base)]
    mid = [sq(b + sq(e[k] + e[k + 1])) for k, b in enumerate(base)]
    high = [sq(b + sq(triple[k] - e[k + 1])) for k, b in enumerate(base)]

    def shift(first, second, third, outer, inner):
        scaled = 3.0 * first
        twice = third + third
        total = second * third + scaled * (second + twice)
        return second * (twice * outer + scaled * inner) / total

    found = []
    for i in range(len(e) - 4):
        minus = shift(low[i], mid[i + 1], high[i + 2], s[i], s[i + 1])
        plus = shift(high[i + 3], mid[i + 2], low[i + 1], s[i + 2], s[i + 1])
        found.append((minus, plus))
    return found


def line_terms(v):
    d = [b - a for a, b in zip(v, v[1:])]
    e = [b - a for a, b in zip(d, d[1:])]
    t = [b - a for a, b in zip(e, e[1:])]
    s = [b - a for a, b in zip(t, t[1:])]
    terms = []
    for i, (minus, plus) in enumerate(corrections(e, t, s)):
        both = 6.0 * (d[i + 2] + d[i + 3]) + (e[i + 1] - e[i + 3]) + (plus - minus)
        terms.append((both, (plus + minus) - s[i + 1]))
    return terms


LANES = 128


def flat_kernel(u_ref, edge_ref, sin_ref, ham_ref, damp_ref, wide_ref):
    rows_x, rows_h, rows_y = u_ref.shape
    step = rows_h // 8
    tiles = rows_y // LANES
    lane = lax.broadcasted_iota(jnp.int32, (8, LANES), 1)

    def one_row(x, _):
        for c in range(tiles):
            cols = pl.ds(c * LANES, LANES)
            wide_ref[c, 8 : 8 + rows_h, :] = u_ref[x, :, cols]
            wide_ref[c, 5:8, :] = edge_ref[x, 3:6, cols]
            wide_ref[c, 8 + rows_h : 11 + rows_h, :] = edge_ref[x, 0:3, cols]
        for c in range(tiles):
            v = [wide_ref[c, pl.ds(8 + j, 8, stride=step), :] for j in range(-3, step + 3)]
            terms = line_terms(v)
            for j in range(step):
                mine = v[j + 3]

                def moved(k):
                    if k == 0:
                        return mine
                    near = pltpu.roll(mine, (-k) % LANES, 1)
                    other = c - 1 if k < 0 else c + 1
                    if 0 <= other < tiles:
                        far = pltpu.roll(wide_ref[other, pl.ds(8 + j, 8, stride=step), :], (-k) % LANES, 1)
                    else:
                        far = jnp.zeros_like(near)
                    inside = lane >= -k if k < 0 else lane < LANES - k
                    return jnp.where(inside, near, far)

                ((both_y, gap_y),) = line_terms([moved(k) for k in range(-3, 4)])
                both_h, gap_h = terms[j]
                sine = sin_ref[pl.ds(j, 8, stride=step), :]
                rows = pl.ds(j, 8, stride=step)
                ham_ref[x * tiles + c, rows, :] = sine * both_y - jnp.abs(both_h)
                damp_ref[x * tiles + c, rows, :] = jnp.abs(sine) * gap_y + gap_h
        return 0

    lax.fori_loop(0, rows_x, one_row, 0)


def side_kernel(own, kept, parity_ref, step_ref, u_ref, even_ref, odd_ref, ham_ref, damp_ref, cos_ref, first_ref, out_ref):
    rows_x, rows_h, rows_y = u_ref.shape
    flipped = parity_ref[0] == 1
    factor = step_ref[0] * (1.0 / 12.0)
    tiles = rows_y // LANES
    for c in range(tiles):
        cols = pl.ds(c * LANES, LANES)

        def one_group(k, _):
            rows = pl.ds(pl.multiple_of(k * 8, 8), 8)
            even = [even_ref[x, rows, cols] for x in range(rows_x)]
            odd = [odd_ref[x, rows, cols] for x in range(rows_x)]
            mine = [u_ref[x, rows, cols] for x in range(rows_x)]
            left = [jnp.where(flipped, a, b) for a, b in zip(even, odd)]
            right = [jnp.where(flipped, b, a) for a, b in zip(even, odd)]
            cosine = cos_ref[rows, :]
            size = jnp.abs(cosine)
            for x, (both, gap) in enumerate(line_terms(left + mine + right)):
                ham = ham_ref[x * tiles + c, rows, :] + cosine * both
                damp = damp_ref[x * tiles + c, rows, :] + size * gap
                moved = mine[x] + factor * (damp + jnp.minimum(0.0, ham))
                out_ref[x, rows, cols] = own * first_ref[x, rows, cols] + kept * moved if own else moved
            return 0

        lax.fori_loop(0, rows_h // 8, one_group, 0, unroll=5)


def on_device(level_set, step_length):
    rows_x, rows_h, rows_y = level_set.shape
    count = lax.axis_size("ha")
    even_pairs = [p for j in range(0, count - 1, 2) for p in ((j, j + 1), (j + 1, j))]
    odd_pairs = [p for j in range(1, count - 1, 2) for p in ((j, j + 1), (j + 1, j))]
    place = lax.axis_index("ha")
    parity = (place % 2).astype(jnp.int32).reshape(1)
    total_h = lax.axis_size("gx") * rows_h
    global_h = lax.axis_index("gx") * rows_h + jnp.arange(rows_h, dtype=jnp.int32)
    heading = 2.0 * jnp.pi * global_h.astype(jnp.float32) / total_h
    cos_grid = jnp.broadcast_to(jnp.cos(heading)[:, None], (rows_h, LANES))
    sin_grid = jnp.broadcast_to(jnp.sin(heading)[:, None], (rows_h, LANES))
    vmem = pl.BlockSpec(memory_space=pltpu.VMEM)
    smem = pl.BlockSpec(memory_space=pltpu.SMEM)
    block = jax.ShapeDtypeStruct(level_set.shape, jnp.float32)
    half = jax.ShapeDtypeStruct((rows_x * rows_y // LANES, rows_h, LANES), jnp.float32)
    cells = rows_x * rows_h * rows_y

    def even(cells):
        return lax.ppermute(cells, "ha", even_pairs)

    def odd(cells):
        return lax.ppermute(cells, "ha", odd_pairs)

    def turn(field):
        edges = jnp.concatenate([field[:, :3], field[:, -3:]], axis=1)
        return lax.ppermute(edges, "gx", [(0, 1), (1, 0)])

    def flat(field, edges):
        return pl.pallas_call(
            flat_kernel,
            out_shape=(half, half),
            in_specs=[vmem] * 3,
            out_specs=(vmem, vmem),
            scratch_shapes=[pltpu.VMEM((rows_y // LANES, rows_h + 16, LANES), jnp.float32)],
            compiler_params=pltpu.CompilerParams(vmem_limit_bytes=4 << 20),
            cost_estimate=pl.CostEstimate(flops=150 * cells, bytes_accessed=12 * cells, transcendentals=4 * cells),
        )(field, edges, sin_grid)

    def section(field, beside_e, beside_o, terms, own, kept):
        return pl.pallas_call(
            functools.partial(side_kernel, own, kept),
            out_shape=block,
            in_specs=[smem] * 2 + [vmem] * 7,
            out_specs=vmem,
            compiler_params=pltpu.CompilerParams(vmem_limit_bytes=6 << 20),
            cost_estimate=pl.CostEstimate(flops=70 * cells, bytes_accessed=28 * cells, transcendentals=2 * cells),
        )(parity, step_length, field, beside_e, beside_o, *terms, cos_grid, level_set)

    def advance(field, own, kept):
        beside_o = odd(field)
        beside_e = even(field)
        terms = flat(field, turn(field))
        return section(field, beside_e, beside_o, terms, own, kept)

    one = advance(level_set, 0.0, 1.0)
    two = advance(one, 0.75, 0.25)
    return advance(two, 1.0 / 3.0, 2.0 / 3.0)


def solution(mesh):
    return jax.shard_map(
        on_device,
        mesh=mesh,
        in_specs=(P("ha", "gx", None), P()),
        out_specs=P("ha", "gx", None),
        check_vma=False,
    )
```

time: 61.7 us -> 47.3 us (0.77)
  the two profiles are of different devices: /device:TPU:257 before, /device:TPU:256 now
where the time goes in v2:
time: 47.3 us; the launch traced here: 46.9 us
  starting transfers between devices  29.6 us (63%)
  waiting for transfers between devices  7.59 us (16%)
  Pallas kernels  6.95 us (15%)
  local copies, waits for them, and re-layouts  1.9 us (4%)
  between operations  0.81 us (2%)
    ppermute x3, starting transfers between devices, odd(): return lax.ppermute(cells, 'ha', odd_pairs)  18.1 us
    ppermute x3, starting transfers between devices, even(): return lax.ppermute(cells, 'ha', even_pairs)  5.76 us
    ppermute x3, starting transfers between devices, turn(): return lax.ppermute(edges, 'gx', [(0, 1), (1, 0)])  5.76 us
    pallas_call x3, Pallas kernels, flat(): pl.pallas_call(flat_kernel, out_shape=(half, half), in_specs=[vmem] * 3,...  4.27 us
    ppermute x3, waiting for transfers between devices, odd(): return lax.ppermute(cells, 'ha', odd_pairs)  3.54 us
    ppermute x3, waiting for transfers between devices, turn(): return lax.ppermute(edges, 'gx', [(0, 1), (1, 0)])  2.77 us
    pallas_call x3, Pallas kernels, section(): pl.pallas_call(functools.partial(side_kernel, own, kept), out_shape=block...  2.68 us
    ppermute x3, waiting for transfers between devices, even(): return lax.ppermute(cells, 'ha', even_pairs)  1.28 us
  transfers between devices with their start and end apart: 9, of which 8 were waited for; matrix products, arithmetic and copies ran while one was open for 2% of the time, Pallas kernels for 9%

profile of v2, /device:TPU:256, one launch (start us, length us, event | category | flops | bytes accessed | tf_op | source)
XLA Modules:
  0.0 46.9 jit_solution(7571979246228527027)
XLA Ops:
  0.0 6.7 %collective-permute-start.1 = (f32[3,80,256]{2,1,0:T(8,128)}, f32[3,80,256]{2,1,0:T(8,128)S(1)}, u32[]{:S(2)}, u32[]{:S(2)}) collective-permute-start(f32[3,80,256]{2,1,0:T(8,128)} %first_ref.5), channel_id=1, source_target_pairs={{1,2},{2,1},{3,4},{4,3},{5,6},{6,5},{7,8},{8,7},{9,10},{10,9},{11,... | collective-permute-start | bytes 737288 | tf_op jit(solution)/shard_map/ppermute | solution.py:141
  6.7 1.9 %collective-permute-start = (f32[3,80,256]{2,1,0:T(8,128)}, f32[3,80,256]{2,1,0:T(8,128)S(1)}, u32[]{:S(2)}, u32[]{:S(2)}) collective-permute-start(f32[3,80,256]{2,1,0:T(8,128)} %first_ref.5), channel_id=1, source_target_pairs={{0,1},{1,0},{2,3},{3,2},{4,5},{5,4},{6,7},{7,6},{8,9},{9,8},{10,11... | collective-permute-start | bytes 737288 | tf_op jit(solution)/shard_map/ppermute | solution.py:138
  8.6 0.8 %fusion.4 = (f32[3,3,256]{2,1,0:T(4,128)S(1)}, f32[3,3,256]{2,1,0:T(4,128)S(1)}) fusion(f32[3,80,256]{2,1,0:T(8,128)} %first_ref.5), kind=kLoop, calls=%fused_computation.8 | loop fusion | bytes 36864 | tf_op jit(solution)/shard_map/slice | solution.py:144
  9.4 1.9 %collective-permute-start.2 = (f32[3,6,256]{2,1,0:T(8,128)S(1)}, f32[3,6,256]{2,1,0:T(8,128)S(1)}, u32[]{:S(2)}, u32[]{:S(2)}) collective-permute-start(f32[3,6,256]{2,1,0:T(8,128)S(1)} %pad_maximum_fusion), channel_id=1, source_target_pairs={{0,256},{256,0},{1,257},{257,1},{2,258},{258,2},{3,259},{259,3},{4... | collective-permute-start | bytes 55304 | tf_op jit(solution)/shard_map/ppermute | solution.py:145
  12.0 0.5 collective-permute-done.2.edge_ref
  12.5 0.1 broadcast_in_dim.4.sin_ref
  12.6 0.0 copy-start
  12.6 0.9 %copy-done = f32[3,80,256]{2,1,0:T(8,128)S(1)} copy-done((f32[3,80,256]{2,1,0:T(8,128)S(1)}, f32[3,80,256]{2,1,0:T(8,128)}, u32[]{:S(2)}) %copy-start) | copy-done | bytes 245784
  13.5 0.0 copy-start.1
  13.5 1.4 %shard_map.28 = (f32[6,80,128]{2,1,0:T(8,128)S(1)}, f32[6,80,128]{2,1,0:T(8,128)S(1)}) custom-call(f32[3,80,256]{2,1,0:T(8,128)S(1)} %copy-done, f32[3,6,256]{2,1,0:T(8,128)S(1)} %collective-permute-done.2.edge_ref, f32[80,128]{1,0:T(8,128)S(1)} %broadcast_in_dim.4.sin_ref), custom_call_target="tpu_custom_call" | custom-call | flops 9216000 | bytes 737280 | tf_op jit(solution)/shard_map/pallas_call | solution.py:148
  14.9 0.3 collective-permute-done.1.odd_ref
  15.2 1.0 %collective-permute-done.even_ref = f32[3,80,256]{2,1,0:T(8,128)S(1)} collective-permute-done((f32[3,80,256]{2,1,0:T(8,128)}, f32[3,80,256]{2,1,0:T(8,128)S(1)}, u32[]{:S(2)}, u32[]{:S(2)}) %collective-permute-start) | collective-permute-done | bytes 245792 | tf_op jit(solution)/shard_map/ppermute | solution.py:138
  16.2 0.1 broadcast_in_dim.5.cos_ref
  16.3 0.0 copy-done.1
  16.3 0.7 %shard_map.29.u_ref = f32[3,80,256]{2,1,0:T(8,128)S(1)} custom-call(s32[1]{0:T(128)} %bitcast.parity_ref, f32[1]{0:T(128)S(6)} %copy.3.step_ref, f32[3,80,256]{2,1,0:T(8,128)S(1)} %copy-done.1, f32[3,80,256]{2,1,0:T(8,128)S(1)} %collective-permute-done.even_ref, f32[3,80,256]{2,1,0:T(8,128)S(1)} %collective-permute-done.1.odd_ref, ...), custom_call_target="tpu_custom_call" | custom-call | flops 4300800 | bytes 1720320 | tf_op jit(solution)/shard_map/pallas_call | solution.py:159
  16.9 5.7 %collective-permute-start.4 = (f32[3,80,256]{2,1,0:T(8,128)S(1)}, f32[3,80,256]{2,1,0:T(8,128)S(1)}, u32[]{:S(2)}, u32[]{:S(2)}) collective-permute-start(f32[3,80,256]{2,1,0:T(8,128)S(1)} %shard_map.29.u_ref), channel_id=1, source_target_pairs={{1,2},{2,1},{3,4},{4,3},{5,6},{6,5},{7,8},{8,7},{9,10},{10,9},{11,... | collective-permute-start | bytes 737288 | tf_op jit(solution)/shard_map/ppermute | solution.py:141
  22.6 1.9 %collective-permute-start.3 = (f32[3,80,256]{2,1,0:T(8,128)S(1)}, f32[3,80,256]{2,1,0:T(8,128)S(1)}, u32[]{:S(2)}, u32[]{:S(2)}) collective-permute-start(f32[3,80,256]{2,1,0:T(8,128)S(1)} %shard_map.29.u_ref), channel_id=1, source_target_pairs={{0,1},{1,0},{2,3},{3,2},{4,5},{5,4},{6,7},{7,6},{8,9},{9,8},{10,11... | collective-permute-start | bytes 737288 | tf_op jit(solution)/shard_map/ppermute | solution.py:138
  24.6 1.9 %collective-permute-start.5 = (f32[3,6,256]{2,1,0:T(8,128)S(1)}, f32[3,6,256]{2,1,0:T(8,128)S(1)}, u32[]{:S(2)}, u32[]{:S(2)}) collective-permute-start(f32[3,6,256]{2,1,0:T(8,128)S(1)} %pad_maximum_fusion.1), channel_id=1, source_target_pairs={{0,256},{256,0},{1,257},{257,1},{2,258},{258,2},{3,259},{259,3},{4... | collective-permute-start | bytes 55304 | tf_op jit(solution)/shard_map/ppermute | solution.py:145
  26.5 1.2 %collective-permute-done.5.edge_ref = f32[3,6,256]{2,1,0:T(8,128)S(1)} collective-permute-done((f32[3,6,256]{2,1,0:T(8,128)S(1)}, f32[3,6,256]{2,1,0:T(8,128)S(1)}, u32[]{:S(2)}, u32[]{:S(2)}) %collective-permute-start.5) | collective-permute-done | bytes 18464 | tf_op jit(solution)/shard_map/ppermute | solution.py:145
  27.7 1.4 %shard_map.30 = (f32[6,80,128]{2,1,0:T(8,128)S(1)}, f32[6,80,128]{2,1,0:T(8,128)S(1)}) custom-call(f32[3,80,256]{2,1,0:T(8,128)S(1)} %shard_map.29.u_ref, f32[3,6,256]{2,1,0:T(8,128)S(1)} %collective-permute-done.5.edge_ref, f32[80,128]{1,0:T(8,128)S(1)} %broadcast_in_dim.4.sin_ref), custom_call_target="tpu_custom_call" | custom-call | flops 9216000 | bytes 737280 | tf_op jit(solution)/shard_map/pallas_call | solution.py:148
  29.1 1.9 %collective-permute-done.4.odd_ref = f32[3,80,256]{2,1,0:T(8,128)S(1)} collective-permute-done((f32[3,80,256]{2,1,0:T(8,128)S(1)}, f32[3,80,256]{2,1,0:T(8,128)S(1)}, u32[]{:S(2)}, u32[]{:S(2)}) %collective-permute-start.4) | collective-permute-done | bytes 245792 | tf_op jit(solution)/shard_map/ppermute | solution.py:141
  31.0 0.0 collective-permute-done.3.even_ref
  31.1 0.7 %shard_map.31.u_ref = f32[3,80,256]{2,1,0:T(8,128)S(1)} custom-call(s32[1]{0:T(128)} %bitcast.parity_ref, f32[1]{0:T(128)S(6)} %copy.3.step_ref, f32[3,80,256]{2,1,0:T(8,128)S(1)} %shard_map.29.u_ref, f32[3,80,256]{2,1,0:T(8,128)S(1)} %collective-permute-done.3.even_ref, f32[3,80,256]{2,1,0:T(8,128)S(1)} %collective-permute-done.4.odd_ref, ...), custom_call_target="tpu_custom_call" | custom-call | flops 4300800 | bytes 1720320 | tf_op jit(solution)/shard_map/pallas_call | solution.py:159
  31.8 5.7 %collective-permute-start.7 = (f32[3,80,256]{2,1,0:T(8,128)S(1)}, f32[3,80,256]{2,1,0:T(8,128)S(1)}, u32[]{:S(2)}, u32[]{:S(2)}) collective-permute-start(f32[3,80,256]{2,1,0:T(8,128)S(1)} %shard_map.31.u_ref), channel_id=1, source_target_pairs={{1,2},{2,1},{3,4},{4,3},{5,6},{6,5},{7,8},{8,7},{9,10},{10,9},{11,... | collective-permute-start | bytes 737288 | tf_op jit(solution)/shard_map/ppermute | solution.py:141
  37.5 1.9 %collective-permute-start.6 = (f32[3,80,256]{2,1,0:T(8,128)S(1)}, f32[3,80,256]{2,1,0:T(8,128)S(1)}, u32[]{:S(2)}, u32[]{:S(2)}) collective-permute-start(f32[3,80,256]{2,1,0:T(8,128)S(1)} %shard_map.31.u_ref), channel_id=1, source_target_pairs={{0,1},{1,0},{2,3},{3,2},{4,5},{5,4},{6,7},{7,6},{8,9},{9,8},{10,11... | collective-permute-start | bytes 737288 | tf_op jit(solution)/shard_map/ppermute | solution.py:138
  39.4 1.9 %collective-permute-start.8 = (f32[3,6,256]{2,1,0:T(8,128)S(1)}, f32[3,6,256]{2,1,0:T(8,128)S(1)}, u32[]{:S(2)}, u32[]{:S(2)}) collective-permute-start(f32[3,6,256]{2,1,0:T(8,128)S(1)} %pad_maximum_fusion.2), channel_id=1, source_target_pairs={{0,256},{256,0},{1,257},{257,1},{2,258},{258,2},{3,259},{259,3},{4... | collective-permute-start | bytes 55304 | tf_op jit(solution)/shard_map/ppermute | solution.py:145
  41.4 1.2 %collective-permute-done.8.edge_ref = f32[3,6,256]{2,1,0:T(8,128)S(1)} collective-permute-done((f32[3,6,256]{2,1,0:T(8,128)S(1)}, f32[3,6,256]{2,1,0:T(8,128)S(1)}, u32[]{:S(2)}, u32[]{:S(2)}) %collective-permute-start.8) | collective-permute-done | bytes 18464 | tf_op jit(solution)/shard_map/ppermute | solution.py:145
  42.5 1.4 %shard_map.32 = (f32[6,80,128]{2,1,0:T(8,128)S(1)}, f32[6,80,128]{2,1,0:T(8,128)S(1)}) custom-call(f32[3,80,256]{2,1,0:T(8,128)S(1)} %shard_map.31.u_ref, f32[3,6,256]{2,1,0:T(8,128)S(1)} %collective-permute-done.8.edge_ref, f32[80,128]{1,0:T(8,128)S(1)} %broadcast_in_dim.4.sin_ref), custom_call_target="tpu_custom_call" | custom-call | flops 9216000 | bytes 737280 | tf_op jit(solution)/shard_map/pallas_call | solution.py:148
  43.9 1.3 %collective-permute-done.7.odd_ref = f32[3,80,256]{2,1,0:T(8,128)S(1)} collective-permute-done((f32[3,80,256]{2,1,0:T(8,128)S(1)}, f32[3,80,256]{2,1,0:T(8,128)S(1)}, u32[]{:S(2)}, u32[]{:S(2)}) %collective-permute-start.7) | collective-permute-done | bytes 245792 | tf_op jit(solution)/shard_map/ppermute | solution.py:141
  45.3 0.3 collective-permute-done.6.even_ref
  45.6 1.4 %shard_map.33 = f32[3,80,256]{2,1,0:T(8,128)} custom-call(s32[1]{0:T(128)} %bitcast.parity_ref, f32[1]{0:T(128)S(6)} %copy.3.step_ref, f32[3,80,256]{2,1,0:T(8,128)S(1)} %shard_map.31.u_ref, f32[3,80,256]{2,1,0:T(8,128)S(1)} %collective-permute-done.6.even_ref, f32[3,80,256]{2,1,0:T(8,128)S(1)} %collective-permute-done.7.odd_ref, ...), custom_call_target="tpu_custom_call" | custom-call | flops 4300800 | bytes 1720320 | tf_op jit(solution)/shard_map/pallas_call | solution.py:159
  (6 shorter events, 0.1 us)
Async XLA Ops:
  0.0 15.2 %collective-permute-start.1 = (f32[3,80,256]{2,1,0:T(8,128)}, f32[3,80,256]{2,1,0:T(8,128)S(1)}, u32[]{:S(2)}, u32[]{:S(2)}) collective-permute-start(f32[3,80,256]{2,1,0:T(8,128)} %first_ref.5), channel_id=1, source_target_pairs={{1,2},{2,1},{3,4},{4,3},{5,6},{6,5},{7,8},{8,7},{9,10},{10,9},{11,... | collective-permute-start | bytes 737288 | tf_op jit(solution)/shard_map/ppermute | solution.py:141
  6.7 9.5 %collective-permute-start = (f32[3,80,256]{2,1,0:T(8,128)}, f32[3,80,256]{2,1,0:T(8,128)S(1)}, u32[]{:S(2)}, u32[]{:S(2)}) collective-permute-start(f32[3,80,256]{2,1,0:T(8,128)} %first_ref.5), channel_id=1, source_target_pairs={{0,1},{1,0},{2,3},{3,2},{4,5},{5,4},{6,7},{7,6},{8,9},{9,8},{10,11... | collective-permute-start | bytes 737288 | tf_op jit(solution)/shard_map/ppermute | solution.py:138
  9.4 3.1 %collective-permute-start.2 = (f32[3,6,256]{2,1,0:T(8,128)S(1)}, f32[3,6,256]{2,1,0:T(8,128)S(1)}, u32[]{:S(2)}, u32[]{:S(2)}) collective-permute-start(f32[3,6,256]{2,1,0:T(8,128)S(1)} %pad_maximum_fusion), channel_id=1, source_target_pairs={{0,256},{256,0},{1,257},{257,1},{2,258},{258,2},{3,259},{259,3},{4... | collective-permute-start | bytes 55304 | tf_op jit(solution)/shard_map/ppermute | solution.py:145
  12.6 1.0 %copy-start = (f32[3,80,256]{2,1,0:T(8,128)S(1)}, f32[3,80,256]{2,1,0:T(8,128)}, u32[]{:S(2)}) copy-start(f32[3,80,256]{2,1,0:T(8,128)} %first_ref.5) | copy-start | bytes 737284
  13.5 2.7 %copy-start.1 = (f32[3,80,256]{2,1,0:T(8,128)S(1)}, f32[3,80,256]{2,1,0:T(8,128)}, u32[]{:S(2)}) copy-start(f32[3,80,256]{2,1,0:T(8,128)} %first_ref.5) | copy-start | bytes 737284
  16.9 14.1 %collective-permute-start.4 = (f32[3,80,256]{2,1,0:T(8,128)S(1)}, f32[3,80,256]{2,1,0:T(8,128)S(1)}, u32[]{:S(2)}, u32[]{:S(2)}) collective-permute-start(f32[3,80,256]{2,1,0:T(8,128)S(1)} %shard_map.29.u_ref), channel_id=1, source_target_pairs={{1,2},{2,1},{3,4},{4,3},{5,6},{6,5},{7,8},{8,7},{9,10},{10,9},{11,... | collective-permute-start | bytes 737288 | tf_op jit(solution)/shard_map/ppermute | solution.py:141
  22.6 8.5 %collective-permute-start.3 = (f32[3,80,256]{2,1,0:T(8,128)S(1)}, f32[3,80,256]{2,1,0:T(8,128)S(1)}, u32[]{:S(2)}, u32[]{:S(2)}) collective-permute-start(f32[3,80,256]{2,1,0:T(8,128)S(1)} %shard_map.29.u_ref), channel_id=1, source_target_pairs={{0,1},{1,0},{2,3},{3,2},{4,5},{5,4},{6,7},{7,6},{8,9},{9,8},{10,11... | collective-permute-start | bytes 737288 | tf_op jit(solution)/shard_map/ppermute | solution.py:138
  24.6 3.1 %collective-permute-start.5 = (f32[3,6,256]{2,1,0:T(8,128)S(1)}, f32[3,6,256]{2,1,0:T(8,128)S(1)}, u32[]{:S(2)}, u32[]{:S(2)}) collective-permute-start(f32[3,6,256]{2,1,0:T(8,128)S(1)} %pad_maximum_fusion.1), channel_id=1, source_target_pairs={{0,256},{256,0},{1,257},{257,1},{2,258},{258,2},{3,259},{259,3},{4... | collective-permute-start | bytes 55304 | tf_op jit(solution)/shard_map/ppermute | solution.py:145
  31.8 13.5 %collective-permute-start.7 = (f32[3,80,256]{2,1,0:T(8,128)S(1)}, f32[3,80,256]{2,1,0:T(8,128)S(1)}, u32[]{:S(2)}, u32[]{:S(2)}) collective-permute-start(f32[3,80,256]{2,1,0:T(8,128)S(1)} %shard_map.31.u_ref), channel_id=1, source_target_pairs={{1,2},{2,1},{3,4},{4,3},{5,6},{6,5},{7,8},{8,7},{9,10},{10,9},{11,... | collective-permute-start | bytes 737288 | tf_op jit(solution)/shard_map/ppermute | solution.py:141
  37.5 8.1 %collective-permute-start.6 = (f32[3,80,256]{2,1,0:T(8,128)S(1)}, f32[3,80,256]{2,1,0:T(8,128)S(1)}, u32[]{:S(2)}, u32[]{:S(2)}) collective-permute-start(f32[3,80,256]{2,1,0:T(8,128)S(1)} %shard_map.31.u_ref), channel_id=1, source_target_pairs={{0,1},{1,0},{2,3},{3,2},{4,5},{5,4},{6,7},{7,6},{8,9},{9,8},{10,11... | collective-permute-start | bytes 737288 | tf_op jit(solution)/shard_map/ppermute | solution.py:138
  39.4 3.1 %collective-permute-start.8 = (f32[3,6,256]{2,1,0:T(8,128)S(1)}, f32[3,6,256]{2,1,0:T(8,128)S(1)}, u32[]{:S(2)}, u32[]{:S(2)}) collective-permute-start(f32[3,6,256]{2,1,0:T(8,128)S(1)} %pad_maximum_fusion.2), channel_id=1, source_target_pairs={{0,256},{256,0},{1,257},{257,1},{2,258},{258,2},{3,259},{259,3},{4... | collective-permute-start | bytes 55304 | tf_op jit(solution)/shard_map/ppermute | solution.py:145

commit v3 on v2

--- a/solution.py
+++ b/solution.py
@@ -48,13 +48,15 @@
 LANES = 128
 
 
-def flat_kernel(u_ref, edge_ref, sin_ref, ham_ref, damp_ref, wide_ref):
+def flat_kernel(own, kept, step_ref, u_ref, edge_ref, sin_ref, first_ref, ham_ref, damp_ref, base_ref, wide_ref):
     rows_x, rows_h, rows_y = u_ref.shape
     step = rows_h // 8
     tiles = rows_y // LANES
     lane = lax.broadcasted_iota(jnp.int32, (8, LANES), 1)
+    factor = step_ref[0] * (kept / 12.0)
 
     def one_row(x, _):
+        base_ref[x] = own * first_ref[x] + kept * u_ref[x] if own else u_ref[x]
         for c in range(tiles):
             cols = pl.ds(c * LANES, LANES)
             wide_ref[c, 8 : 8 + rows_h, :] = u_ref[x, :, cols]
@@ -82,17 +84,17 @@
                 both_h, gap_h = terms[j]
                 sine = sin_ref[pl.ds(j, 8, stride=step), :]
                 rows = pl.ds(j, 8, stride=step)
-                ham_ref[x * tiles + c, rows, :] = sine * both_y - jnp.abs(both_h)
-                damp_ref[x * tiles + c, rows, :] = jnp.abs(sine) * gap_y + gap_h
+                ham_ref[x * tiles + c, rows, :] = factor * (sine * both_y - jnp.abs(both_h))
+                damp_ref[x * tiles + c, rows, :] = factor * (jnp.abs(sine) * gap_y + gap_h)
         return 0
 
     lax.fori_loop(0, rows_x, one_row, 0)
 
 
-def side_kernel(own, kept, parity_ref, step_ref, u_ref, even_ref, odd_ref, ham_ref, damp_ref, cos_ref, first_ref, out_ref):
+def side_kernel(kept, parity_ref, step_ref, u_ref, even_ref, odd_ref, ham_ref, damp_ref, base_ref, cos_ref, out_ref):
     rows_x, rows_h, rows_y = u_ref.shape
     flipped = parity_ref[0] == 1
-    factor = step_ref[0] * (1.0 / 12.0)
+    factor = step_ref[0] * (kept / 12.0)
     tiles = rows_y // LANES
     for c in range(tiles):
         cols = pl.ds(c * LANES, LANES)
@@ -104,13 +106,12 @@
             mine = [u_ref[x, rows, cols] for x in range(rows_x)]
             left = [jnp.where(flipped, a, b) for a, b in zip(even, odd)]
             right = [jnp.where(flipped, b, a) for a, b in zip(even, odd)]
-            cosine = cos_ref[rows, :]
+            cosine = factor * cos_ref[rows, :]
             size = jnp.abs(cosine)
             for x, (both, gap) in enumerate(line_terms(left + mine + right)):
                 ham = ham_ref[x * tiles + c, rows, :] + cosine * both
                 damp = damp_ref[x * tiles + c, rows, :] + size * gap
-                moved = mine[x] + factor * (damp + jnp.minimum(0.0, ham))
-                out_ref[x, rows, cols] = own * first_ref[x, rows, cols] + kept * moved if own else moved
+                out_ref[x, rows, cols] = base_ref[x, rows, cols] + (damp + jnp.minimum(0.0, ham))
             return 0
 
         lax.fori_loop(0, rows_h // 8, one_group, 0, unroll=5)
@@ -144,32 +145,32 @@
         edges = jnp.concatenate([field[:, :3], field[:, -3:]], axis=1)
         return lax.ppermute(edges, "gx", [(0, 1), (1, 0)])
 
-    def flat(field, edges):
+    def flat(field, edges, own, kept):
         return pl.pallas_call(
-            flat_kernel,
-            out_shape=(half, half),
-            in_specs=[vmem] * 3,
-            out_specs=(vmem, vmem),
+            functools.partial(flat_kernel, own, kept),
+            out_shape=(half, half, block),
+            in_specs=[smem] + [vmem] * 4,
+            out_specs=(vmem, vmem, vmem),
             scratch_shapes=[pltpu.VMEM((rows_y // LANES, rows_h + 16, LANES), jnp.float32)],
             compiler_params=pltpu.CompilerParams(vmem_limit_bytes=4 << 20),
             cost_estimate=pl.CostEstimate(flops=150 * cells, bytes_accessed=12 * cells, transcendentals=4 * cells),
-        )(field, edges, sin_grid)
+        )(step_length, field, edges, sin_grid, level_set)
 
-    def section(field, beside_e, beside_o, terms, own, kept):
+    def section(field, beside_e, beside_o, terms, kept):
         return pl.pallas_call(
-            functools.partial(side_kernel, own, kept),
+            functools.partial(side_kernel, kept),
             out_shape=block,
             in_specs=[smem] * 2 + [vmem] * 7,
             out_specs=vmem,
             compiler_params=pltpu.CompilerParams(vmem_limit_bytes=6 << 20),
             cost_estimate=pl.CostEstimate(flops=70 * cells, bytes_accessed=28 * cells, transcendentals=2 * cells),
-        )(parity, step_length, field, beside_e, beside_o, *terms, cos_grid, level_set)
+        )(parity, step_length, field, beside_e, beside_o, *terms, cos_grid)
 
     def advance(field, own, kept):
         beside_o = odd(field)
         beside_e = even(field)
-        terms = flat(field, turn(field))
-        return section(field, beside_e, beside_o, terms, own, kept)
+        terms = flat(field, turn(field), own, kept)
+        return section(field, beside_e, beside_o, terms, kept)
 
     one = advance(level_set, 0.0, 1.0)
     two = advance(one, 0.75, 0.25)

time: 47.3 us -> 47.3 us (level)
  no operation moved by 1% of the time
where the time goes in v3:
time: 47.3 us; the launch traced here: 46.9 us
  starting transfers between devices  29.6 us (63%)
  waiting for transfers between devices  7.49 us (16%)
  Pallas kernels  7.01 us (15%)
  local copies, waits for them, and re-layouts  1.9 us (4%)
  between operations  0.81 us (2%)
    ppermute x3, starting transfers between devices, odd(): return lax.ppermute(cells, 'ha', odd_pairs)  18.1 us
    ppermute x3, starting transfers between devices, even(): return lax.ppermute(cells, 'ha', even_pairs)  5.76 us
    ppermute x3, starting transfers between devices, turn(): return lax.ppermute(edges, 'gx', [(0, 1), (1, 0)])  5.76 us
    pallas_call x3, Pallas kernels, flat(): pl.pallas_call(functools.partial(flat_kernel, own, kept), out_shape=(half...  4.37 us
    ppermute x3, waiting for transfers between devices, odd(): return lax.ppermute(cells, 'ha', odd_pairs)  3.46 us
    ppermute x3, waiting for transfers between devices, turn(): return lax.ppermute(edges, 'gx', [(0, 1), (1, 0)])  2.77 us
    pallas_call x3, Pallas kernels, section(): pl.pallas_call(functools.partial(side_kernel, kept), out_shape=block, in_...  2.64 us
    ppermute x3, waiting for transfers between devices, even(): return lax.ppermute(cells, 'ha', even_pairs)  1.25 us
  transfers between devices with their start and end apart: 9, of which 8 were waited for; matrix products, arithmetic and copies ran while one was open for 2% of the time, Pallas kernels for 9%

profile of v3, /device:TPU:256, one launch (start us, length us, event | category | flops | bytes accessed | tf_op | source)
XLA Modules:
  0.0 46.9 jit_solution(4302697740320607470)
XLA Ops:
  0.0 6.7 %collective-permute-start.1 = (f32[3,80,256]{2,1,0:T(8,128)}, f32[3,80,256]{2,1,0:T(8,128)S(1)}, u32[]{:S(2)}, u32[]{:S(2)}) collective-permute-start(f32[3,80,256]{2,1,0:T(8,128)} %first_ref.5), channel_id=1, source_target_pairs={{1,2},{2,1},{3,4},{4,3},{5,6},{6,5},{7,8},{8,7},{9,10},{10,9},{11,... | collective-permute-start | bytes 737288 | tf_op jit(solution)/shard_map/ppermute | solution.py:142
  6.7 1.9 %collective-permute-start = (f32[3,80,256]{2,1,0:T(8,128)}, f32[3,80,256]{2,1,0:T(8,128)S(1)}, u32[]{:S(2)}, u32[]{:S(2)}) collective-permute-start(f32[3,80,256]{2,1,0:T(8,128)} %first_ref.5), channel_id=1, source_target_pairs={{0,1},{1,0},{2,3},{3,2},{4,5},{5,4},{6,7},{7,6},{8,9},{9,8},{10,11... | collective-permute-start | bytes 737288 | tf_op jit(solution)/shard_map/ppermute | solution.py:139
  8.6 0.8 %fusion.4 = (f32[3,3,256]{2,1,0:T(4,128)S(1)}, f32[3,3,256]{2,1,0:T(4,128)S(1)}) fusion(f32[3,80,256]{2,1,0:T(8,128)} %first_ref.5), kind=kLoop, calls=%fused_computation.8 | loop fusion | bytes 36864 | tf_op jit(solution)/shard_map/slice | solution.py:145
  9.4 1.9 %collective-permute-start.2 = (f32[3,6,256]{2,1,0:T(8,128)S(1)}, f32[3,6,256]{2,1,0:T(8,128)S(1)}, u32[]{:S(2)}, u32[]{:S(2)}) collective-permute-start(f32[3,6,256]{2,1,0:T(8,128)S(1)} %pad_maximum_fusion), channel_id=1, source_target_pairs={{0,256},{256,0},{1,257},{257,1},{2,258},{258,2},{3,259},{259,3},{4... | collective-permute-start | bytes 55304 | tf_op jit(solution)/shard_map/ppermute | solution.py:146
  12.0 0.5 collective-permute-done.2.edge_ref
  12.5 0.1 broadcast_in_dim.4.sin_ref
  12.6 0.0 copy-start
  12.6 0.9 %copy-done = f32[3,80,256]{2,1,0:T(8,128)S(1)} copy-done((f32[3,80,256]{2,1,0:T(8,128)S(1)}, f32[3,80,256]{2,1,0:T(8,128)}, u32[]{:S(2)}) %copy-start) | copy-done | bytes 245784
  13.5 0.0 copy-start.1
  13.5 1.5 %shard_map.28 = (f32[6,80,128]{2,1,0:T(8,128)S(1)}, f32[6,80,128]{2,1,0:T(8,128)S(1)}, f32[3,80,256]{2,1,0:T(8,128)S(1)}) custom-call(f32[1]{0:T(128)S(6)} %copy.3.step_ref, f32[3,80,256]{2,1,0:T(8,128)S(1)} %copy-done, f32[3,6,256]{2,1,0:T(8,128)S(1)} %collective-permute-done.2.edge_ref, f32[80,128]{1,0:T(8,128)S(1)} %broadcast_in_dim.4.sin_ref, ...), custom_call_target="tpu_custom_call" | custom-call | flops 9216000 | bytes 737280 | tf_op jit(solution)/shard_map/pallas_call | solution.py:149
  15.0 0.2 collective-permute-done.1.odd_ref
  15.2 1.0 %collective-permute-done.even_ref = f32[3,80,256]{2,1,0:T(8,128)S(1)} collective-permute-done((f32[3,80,256]{2,1,0:T(8,128)}, f32[3,80,256]{2,1,0:T(8,128)S(1)}, u32[]{:S(2)}, u32[]{:S(2)}) %collective-permute-start) | collective-permute-done | bytes 245792 | tf_op jit(solution)/shard_map/ppermute | solution.py:139
  16.2 0.1 broadcast_in_dim.5.cos_ref
  16.3 0.0 copy-done.1
  16.3 0.7 %shard_map.29.u_ref = f32[3,80,256]{2,1,0:T(8,128)S(1)} custom-call(s32[1]{0:T(128)} %bitcast.parity_ref, f32[1]{0:T(128)S(6)} %copy.3.step_ref, f32[3,80,256]{2,1,0:T(8,128)S(1)} %copy-done.1, f32[3,80,256]{2,1,0:T(8,128)S(1)} %collective-permute-done.even_ref, f32[3,80,256]{2,1,0:T(8,128)S(1)} %collective-permute-done.1.odd_ref, ...), custom_call_target="tpu_custom_call" | custom-call | flops 4300800 | bytes 1720320 | tf_op jit(solution)/shard_map/pallas_call | solution.py:160
  16.9 5.7 %collective-permute-start.4 = (f32[3,80,256]{2,1,0:T(8,128)S(1)}, f32[3,80,256]{2,1,0:T(8,128)S(1)}, u32[]{:S(2)}, u32[]{:S(2)}) collective-permute-start(f32[3,80,256]{2,1,0:T(8,128)S(1)} %shard_map.29.u_ref), channel_id=1, source_target_pairs={{1,2},{2,1},{3,4},{4,3},{5,6},{6,5},{7,8},{8,7},{9,10},{10,9},{11,... | collective-permute-start | bytes 737288 | tf_op jit(solution)/shard_map/ppermute | solution.py:142
  22.6 1.9 %collective-permute-start.3 = (f32[3,80,256]{2,1,0:T(8,128)S(1)}, f32[3,80,256]{2,1,0:T(8,128)S(1)}, u32[]{:S(2)}, u32[]{:S(2)}) collective-permute-start(f32[3,80,256]{2,1,0:T(8,128)S(1)} %shard_map.29.u_ref), channel_id=1, source_target_pairs={{0,1},{1,0},{2,3},{3,2},{4,5},{5,4},{6,7},{7,6},{8,9},{9,8},{10,11... | collective-permute-start | bytes 737288 | tf_op jit(solution)/shard_map/ppermute | solution.py:139
  24.6 1.9 %collective-permute-start.5 = (f32[3,6,256]{2,1,0:T(8,128)S(1)}, f32[3,6,256]{2,1,0:T(8,128)S(1)}, u32[]{:S(2)}, u32[]{:S(2)}) collective-permute-start(f32[3,6,256]{2,1,0:T(8,128)S(1)} %pad_maximum_fusion.1), channel_id=1, source_target_pairs={{0,256},{256,0},{1,257},{257,1},{2,258},{258,2},{3,259},{259,3},{4... | collective-permute-start | bytes 55304 | tf_op jit(solution)/shard_map/ppermute | solution.py:146
  26.5 1.2 %collective-permute-done.5.edge_ref = f32[3,6,256]{2,1,0:T(8,128)S(1)} collective-permute-done((f32[3,6,256]{2,1,0:T(8,128)S(1)}, f32[3,6,256]{2,1,0:T(8,128)S(1)}, u32[]{:S(2)}, u32[]{:S(2)}) %collective-permute-start.5) | collective-permute-done | bytes 18464 | tf_op jit(solution)/shard_map/ppermute | solution.py:146
  27.7 1.5 %shard_map.30 = (f32[6,80,128]{2,1,0:T(8,128)S(1)}, f32[6,80,128]{2,1,0:T(8,128)S(1)}, f32[3,80,256]{2,1,0:T(8,128)S(1)}) custom-call(f32[1]{0:T(128)S(6)} %copy.3.step_ref, f32[3,80,256]{2,1,0:T(8,128)S(1)} %shard_map.29.u_ref, f32[3,6,256]{2,1,0:T(8,128)S(1)} %collective-permute-done.5.edge_ref, f32[80,128]{1,0:T(8,128)S(1)} %broadcast_in_dim.4.sin_ref, ...), custom_call_target="tpu_custom_call" | custom-call | flops 9216000 | bytes 737280 | tf_op jit(solution)/shard_map/pallas_call | solution.py:149
  29.1 1.9 %collective-permute-done.4.odd_ref = f32[3,80,256]{2,1,0:T(8,128)S(1)} collective-permute-done((f32[3,80,256]{2,1,0:T(8,128)S(1)}, f32[3,80,256]{2,1,0:T(8,128)S(1)}, u32[]{:S(2)}, u32[]{:S(2)}) %collective-permute-start.4) | collective-permute-done | bytes 245792 | tf_op jit(solution)/shard_map/ppermute | solution.py:142
  31.1 0.0 collective-permute-done.3.even_ref
  31.1 0.6 %shard_map.31.u_ref = f32[3,80,256]{2,1,0:T(8,128)S(1)} custom-call(s32[1]{0:T(128)} %bitcast.parity_ref, f32[1]{0:T(128)S(6)} %copy.3.step_ref, f32[3,80,256]{2,1,0:T(8,128)S(1)} %shard_map.29.u_ref, f32[3,80,256]{2,1,0:T(8,128)S(1)} %collective-permute-done.3.even_ref, f32[3,80,256]{2,1,0:T(8,128)S(1)} %collective-permute-done.4.odd_ref, ...), custom_call_target="tpu_custom_call" | custom-call | flops 4300800 | bytes 1720320 | tf_op jit(solution)/shard_map/pallas_call | solution.py:160
  31.7 5.7 %collective-permute-start.7 = (f32[3,80,256]{2,1,0:T(8,128)S(1)}, f32[3,80,256]{2,1,0:T(8,128)S(1)}, u32[]{:S(2)}, u32[]{:S(2)}) collective-permute-start(f32[3,80,256]{2,1,0:T(8,128)S(1)} %shard_map.31.u_ref), channel_id=1, source_target_pairs={{1,2},{2,1},{3,4},{4,3},{5,6},{6,5},{7,8},{8,7},{9,10},{10,9},{11,... | collective-permute-start | bytes 737288 | tf_op jit(solution)/shard_map/ppermute | solution.py:142
  37.4 1.9 %collective-permute-start.6 = (f32[3,80,256]{2,1,0:T(8,128)S(1)}, f32[3,80,256]{2,1,0:T(8,128)S(1)}, u32[]{:S(2)}, u32[]{:S(2)}) collective-permute-start(f32[3,80,256]{2,1,0:T(8,128)S(1)} %shard_map.31.u_ref), channel_id=1, source_target_pairs={{0,1},{1,0},{2,3},{3,2},{4,5},{5,4},{6,7},{7,6},{8,9},{9,8},{10,11... | collective-permute-start | bytes 737288 | tf_op jit(solution)/shard_map/ppermute | solution.py:139
  39.4 1.9 %collective-permute-start.8 = (f32[3,6,256]{2,1,0:T(8,128)S(1)}, f32[3,6,256]{2,1,0:T(8,128)S(1)}, u32[]{:S(2)}, u32[]{:S(2)}) collective-permute-start(f32[3,6,256]{2,1,0:T(8,128)S(1)} %pad_maximum_fusion.2), channel_id=1, source_target_pairs={{0,256},{256,0},{1,257},{257,1},{2,258},{258,2},{3,259},{259,3},{4... | collective-permute-start | bytes 55304 | tf_op jit(solution)/shard_map/ppermute | solution.py:146
  41.3 1.2 %collective-permute-done.8.edge_ref = f32[3,6,256]{2,1,0:T(8,128)S(1)} collective-permute-done((f32[3,6,256]{2,1,0:T(8,128)S(1)}, f32[3,6,256]{2,1,0:T(8,128)S(1)}, u32[]{:S(2)}, u32[]{:S(2)}) %collective-permute-start.8) | collective-permute-done | bytes 18464 | tf_op jit(solution)/shard_map/ppermute | solution.py:146
  42.5 1.5 %shard_map.32 = (f32[6,80,128]{2,1,0:T(8,128)S(1)}, f32[6,80,128]{2,1,0:T(8,128)S(1)}, f32[3,80,256]{2,1,0:T(8,128)S(1)}) custom-call(f32[1]{0:T(128)S(6)} %copy.3.step_ref, f32[3,80,256]{2,1,0:T(8,128)S(1)} %shard_map.31.u_ref, f32[3,6,256]{2,1,0:T(8,128)S(1)} %collective-permute-done.8.edge_ref, f32[80,128]{1,0:T(8,128)S(1)} %broadcast_in_dim.4.sin_ref, ...), custom_call_target="tpu_custom_call" | custom-call | flops 9216000 | bytes 737280 | tf_op jit(solution)/shard_map/pallas_call | solution.py:149
  44.0 1.3 %collective-permute-done.7.odd_ref = f32[3,80,256]{2,1,0:T(8,128)S(1)} collective-permute-done((f32[3,80,256]{2,1,0:T(8,128)S(1)}, f32[3,80,256]{2,1,0:T(8,128)S(1)}, u32[]{:S(2)}, u32[]{:S(2)}) %collective-permute-start.7) | collective-permute-done | bytes 245792 | tf_op jit(solution)/shard_map/ppermute | solution.py:142
  45.3 0.3 collective-permute-done.6.even_ref
  45.5 1.3 %shard_map.33 = f32[3,80,256]{2,1,0:T(8,128)} custom-call(s32[1]{0:T(128)} %bitcast.parity_ref, f32[1]{0:T(128)S(6)} %copy.3.step_ref, f32[3,80,256]{2,1,0:T(8,128)S(1)} %shard_map.31.u_ref, f32[3,80,256]{2,1,0:T(8,128)S(1)} %collective-permute-done.6.even_ref, f32[3,80,256]{2,1,0:T(8,128)S(1)} %collective-permute-done.7.odd_ref, ...), custom_call_target="tpu_custom_call" | custom-call | flops 4300800 | bytes 1720320 | tf_op jit(solution)/shard_map/pallas_call | solution.py:160
  (6 shorter events, 0.1 us)
Async XLA Ops:
  0.0 15.2 %collective-permute-start.1 = (f32[3,80,256]{2,1,0:T(8,128)}, f32[3,80,256]{2,1,0:T(8,128)S(1)}, u32[]{:S(2)}, u32[]{:S(2)}) collective-permute-start(f32[3,80,256]{2,1,0:T(8,128)} %first_ref.5), channel_id=1, source_target_pairs={{1,2},{2,1},{3,4},{4,3},{5,6},{6,5},{7,8},{8,7},{9,10},{10,9},{11,... | collective-permute-start | bytes 737288 | tf_op jit(solution)/shard_map/ppermute | solution.py:142
  6.7 9.5 %collective-permute-start = (f32[3,80,256]{2,1,0:T(8,128)}, f32[3,80,256]{2,1,0:T(8,128)S(1)}, u32[]{:S(2)}, u32[]{:S(2)}) collective-permute-start(f32[3,80,256]{2,1,0:T(8,128)} %first_ref.5), channel_id=1, source_target_pairs={{0,1},{1,0},{2,3},{3,2},{4,5},{5,4},{6,7},{7,6},{8,9},{9,8},{10,11... | collective-permute-start | bytes 737288 | tf_op jit(solution)/shard_map/ppermute | solution.py:139
  9.4 3.1 %collective-permute-start.2 = (f32[3,6,256]{2,1,0:T(8,128)S(1)}, f32[3,6,256]{2,1,0:T(8,128)S(1)}, u32[]{:S(2)}, u32[]{:S(2)}) collective-permute-start(f32[3,6,256]{2,1,0:T(8,128)S(1)} %pad_maximum_fusion), channel_id=1, source_target_pairs={{0,256},{256,0},{1,257},{257,1},{2,258},{258,2},{3,259},{259,3},{4... | collective-permute-start | bytes 55304 | tf_op jit(solution)/shard_map/ppermute | solution.py:146
  12.6 1.0 %copy-start = (f32[3,80,256]{2,1,0:T(8,128)S(1)}, f32[3,80,256]{2,1,0:T(8,128)}, u32[]{:S(2)}) copy-start(f32[3,80,256]{2,1,0:T(8,128)} %first_ref.5) | copy-start | bytes 737284
  13.5 2.7 %copy-start.1 = (f32[3,80,256]{2,1,0:T(8,128)S(1)}, f32[3,80,256]{2,1,0:T(8,128)}, u32[]{:S(2)}) copy-start(f32[3,80,256]{2,1,0:T(8,128)} %first_ref.5) | copy-start | bytes 737284
  16.9 14.2 %collective-permute-start.4 = (f32[3,80,256]{2,1,0:T(8,128)S(1)}, f32[3,80,256]{2,1,0:T(8,128)S(1)}, u32[]{:S(2)}, u32[]{:S(2)}) collective-permute-start(f32[3,80,256]{2,1,0:T(8,128)S(1)} %shard_map.29.u_ref), channel_id=1, source_target_pairs={{1,2},{2,1},{3,4},{4,3},{5,6},{6,5},{7,8},{8,7},{9,10},{10,9},{11,... | collective-permute-start | bytes 737288 | tf_op jit(solution)/shard_map/ppermute | solution.py:142
  22.6 8.5 %collective-permute-start.3 = (f32[3,80,256]{2,1,0:T(8,128)S(1)}, f32[3,80,256]{2,1,0:T(8,128)S(1)}, u32[]{:S(2)}, u32[]{:S(2)}) collective-permute-start(f32[3,80,256]{2,1,0:T(8,128)S(1)} %shard_map.29.u_ref), channel_id=1, source_target_pairs={{0,1},{1,0},{2,3},{3,2},{4,5},{5,4},{6,7},{7,6},{8,9},{9,8},{10,11... | collective-permute-start | bytes 737288 | tf_op jit(solution)/shard_map/ppermute | solution.py:139
  24.6 3.1 %collective-permute-start.5 = (f32[3,6,256]{2,1,0:T(8,128)S(1)}, f32[3,6,256]{2,1,0:T(8,128)S(1)}, u32[]{:S(2)}, u32[]{:S(2)}) collective-permute-start(f32[3,6,256]{2,1,0:T(8,128)S(1)} %pad_maximum_fusion.1), channel_id=1, source_target_pairs={{0,256},{256,0},{1,257},{257,1},{2,258},{258,2},{3,259},{259,3},{4... | collective-permute-start | bytes 55304 | tf_op jit(solution)/shard_map/ppermute | solution.py:146
  31.7 13.5 %collective-permute-start.7 = (f32[3,80,256]{2,1,0:T(8,128)S(1)}, f32[3,80,256]{2,1,0:T(8,128)S(1)}, u32[]{:S(2)}, u32[]{:S(2)}) collective-permute-start(f32[3,80,256]{2,1,0:T(8,128)S(1)} %shard_map.31.u_ref), channel_id=1, source_target_pairs={{1,2},{2,1},{3,4},{4,3},{5,6},{6,5},{7,8},{8,7},{9,10},{10,9},{11,... | collective-permute-start | bytes 737288 | tf_op jit(solution)/shard_map/ppermute | solution.py:142
  37.4 8.1 %collective-permute-start.6 = (f32[3,80,256]{2,1,0:T(8,128)S(1)}, f32[3,80,256]{2,1,0:T(8,128)S(1)}, u32[]{:S(2)}, u32[]{:S(2)}) collective-permute-start(f32[3,80,256]{2,1,0:T(8,128)S(1)} %shard_map.31.u_ref), channel_id=1, source_target_pairs={{0,1},{1,0},{2,3},{3,2},{4,5},{5,4},{6,7},{7,6},{8,9},{9,8},{10,11... | collective-permute-start | bytes 737288 | tf_op jit(solution)/shard_map/ppermute | solution.py:139
  39.4 3.1 %collective-permute-start.8 = (f32[3,6,256]{2,1,0:T(8,128)S(1)}, f32[3,6,256]{2,1,0:T(8,128)S(1)}, u32[]{:S(2)}, u32[]{:S(2)}) collective-permute-start(f32[3,6,256]{2,1,0:T(8,128)S(1)} %pad_maximum_fusion.2), channel_id=1, source_target_pairs={{0,256},{256,0},{1,257},{257,1},{2,258},{258,2},{3,259},{259,3},{4... | collective-permute-start | bytes 55304 | tf_op jit(solution)/shard_map/ppermute | solution.py:146

commit v4 on v3

--- a/solution.py
+++ b/solution.py
@@ -48,15 +48,17 @@
 LANES = 128
 
 
-def flat_kernel(own, kept, step_ref, u_ref, edge_ref, sin_ref, first_ref, ham_ref, damp_ref, base_ref, wide_ref):
+def flat_kernel(own, kept, step_ref, u_ref, edge_ref, sin_ref, first_ref, ham_ref, damp_ref, *rest):
     rows_x, rows_h, rows_y = u_ref.shape
+    wide_ref = rest[-1]
     step = rows_h // 8
     tiles = rows_y // LANES
     lane = lax.broadcasted_iota(jnp.int32, (8, LANES), 1)
     factor = step_ref[0] * (kept / 12.0)
 
     def one_row(x, _):
-        base_ref[x] = own * first_ref[x] + kept * u_ref[x] if own else u_ref[x]
+        if own:
+            rest[0][x] = own * first_ref[x] + kept * u_ref[x]
         for c in range(tiles):
             cols = pl.ds(c * LANES, LANES)
             wide_ref[c, 8 : 8 + rows_h, :] = u_ref[x, :, cols]
@@ -146,15 +148,17 @@
         return lax.ppermute(edges, "gx", [(0, 1), (1, 0)])
 
     def flat(field, edges, own, kept):
-        return pl.pallas_call(
+        more = 1 if own else 0
+        found = pl.pallas_call(
             functools.partial(flat_kernel, own, kept),
-            out_shape=(half, half, block),
+            out_shape=(half, half) + (block,) * more,
             in_specs=[smem] + [vmem] * 4,
-            out_specs=(vmem, vmem, vmem),
+            out_specs=(vmem,) * (2 + more),
             scratch_shapes=[pltpu.VMEM((rows_y // LANES, rows_h + 16, LANES), jnp.float32)],
             compiler_params=pltpu.CompilerParams(vmem_limit_bytes=4 << 20),
             cost_estimate=pl.CostEstimate(flops=150 * cells, bytes_accessed=12 * cells, transcendentals=4 * cells),
         )(step_length, field, edges, sin_grid, level_set)
+        return found if own else (*found, field)
 
     def section(field, beside_e, beside_o, terms, kept):
         return pl.pallas_call(

time: 47.3 us -> 47.3 us (level)
  no operation moved by 1% of the time
where the time goes in v4:
time: 47.3 us; the launch traced here: 46.9 us
  starting transfers between devices  29.6 us (63%)
  waiting for transfers between devices  7.5 us (16%)
  Pallas kernels  7 us (15%)
  local copies, waits for them, and re-layouts  1.9 us (4%)
  between operations  0.81 us (2%)
    ppermute x3, starting transfers between devices, odd(): return lax.ppermute(cells, 'ha', odd_pairs)  18.1 us
    ppermute x3, starting transfers between devices, even(): return lax.ppermute(cells, 'ha', even_pairs)  5.76 us
    ppermute x3, starting transfers between devices, turn(): return lax.ppermute(edges, 'gx', [(0, 1), (1, 0)])  5.76 us
    pallas_call x3, Pallas kernels, flat(): pl.pallas_call(functools.partial(flat_kernel, own, kept), out_shape=(half...  4.36 us
    ppermute x3, waiting for transfers between devices, odd(): return lax.ppermute(cells, 'ha', odd_pairs)  3.46 us
    ppermute x3, waiting for transfers between devices, turn(): return lax.ppermute(edges, 'gx', [(0, 1), (1, 0)])  2.77 us
    pallas_call x3, Pallas kernels, section(): pl.pallas_call(functools.partial(side_kernel, kept), out_shape=block, in_...  2.64 us
    ppermute x3, waiting for transfers between devices, even(): return lax.ppermute(cells, 'ha', even_pairs)  1.26 us
  transfers between devices with their start and end apart: 9, of which 8 were waited for; matrix products, arithmetic and copies ran while one was open for 2% of the time, Pallas kernels for 9%

profile of v4, /device:TPU:256, one launch (start us, length us, event | category | flops | bytes accessed | tf_op | source)
XLA Modules:
  0.0 46.9 jit_solution(2956609972116452490)
XLA Ops:
  0.0 6.7 %collective-permute-start.1 = (f32[3,80,256]{2,1,0:T(8,128)}, f32[3,80,256]{2,1,0:T(8,128)S(1)}, u32[]{:S(2)}, u32[]{:S(2)}) collective-permute-start(f32[3,80,256]{2,1,0:T(8,128)} %first_ref.5), channel_id=1, source_target_pairs={{1,2},{2,1},{3,4},{4,3},{5,6},{6,5},{7,8},{8,7},{9,10},{10,9},{11,... | collective-permute-start | bytes 737288 | tf_op jit(solution)/shard_map/ppermute | solution.py:144
  6.7 1.9 %collective-permute-start = (f32[3,80,256]{2,1,0:T(8,128)}, f32[3,80,256]{2,1,0:T(8,128)S(1)}, u32[]{:S(2)}, u32[]{:S(2)}) collective-permute-start(f32[3,80,256]{2,1,0:T(8,128)} %first_ref.5), channel_id=1, source_target_pairs={{0,1},{1,0},{2,3},{3,2},{4,5},{5,4},{6,7},{7,6},{8,9},{9,8},{10,11... | collective-permute-start | bytes 737288 | tf_op jit(solution)/shard_map/ppermute | solution.py:141
  8.6 0.8 %fusion.4 = (f32[3,3,256]{2,1,0:T(4,128)S(1)}, f32[3,3,256]{2,1,0:T(4,128)S(1)}) fusion(f32[3,80,256]{2,1,0:T(8,128)} %first_ref.5), kind=kLoop, calls=%fused_computation.8 | loop fusion | bytes 36864 | tf_op jit(solution)/shard_map/slice | solution.py:147
  9.4 1.9 %collective-permute-start.2 = (f32[3,6,256]{2,1,0:T(8,128)S(1)}, f32[3,6,256]{2,1,0:T(8,128)S(1)}, u32[]{:S(2)}, u32[]{:S(2)}) collective-permute-start(f32[3,6,256]{2,1,0:T(8,128)S(1)} %pad_maximum_fusion), channel_id=1, source_target_pairs={{0,256},{256,0},{1,257},{257,1},{2,258},{258,2},{3,259},{259,3},{4... | collective-permute-start | bytes 55304 | tf_op jit(solution)/shard_map/ppermute | solution.py:148
  12.0 0.5 collective-permute-done.2.edge_ref
  12.5 0.1 broadcast_in_dim.4.sin_ref
  12.6 0.0 copy-start
  12.6 0.9 %copy-done = f32[3,80,256]{2,1,0:T(8,128)S(1)} copy-done((f32[3,80,256]{2,1,0:T(8,128)S(1)}, f32[3,80,256]{2,1,0:T(8,128)}, u32[]{:S(2)}) %copy-start) | copy-done | bytes 245784
  13.5 0.0 copy-start.1
  13.5 1.4 %shard_map.28 = (f32[6,80,128]{2,1,0:T(8,128)S(1)}, f32[6,80,128]{2,1,0:T(8,128)S(1)}) custom-call(f32[1]{0:T(128)S(6)} %copy.3.step_ref, f32[3,80,256]{2,1,0:T(8,128)S(1)} %copy-done, f32[3,6,256]{2,1,0:T(8,128)S(1)} %collective-permute-done.2.edge_ref, f32[80,128]{1,0:T(8,128)S(1)} %broadcast_in_dim.4.sin_ref, f32[3,80,256]{2,1,0:T(8,128)S(1)} %copy-done), custom_call_target="tpu_custom_call" | custom-call | flops 9216000 | bytes 737280 | tf_op jit(solution)/shard_map/pallas_call | solution.py:152
  15.0 0.3 collective-permute-done.1.odd_ref
  15.2 1.0 %collective-permute-done.even_ref = f32[3,80,256]{2,1,0:T(8,128)S(1)} collective-permute-done((f32[3,80,256]{2,1,0:T(8,128)}, f32[3,80,256]{2,1,0:T(8,128)S(1)}, u32[]{:S(2)}, u32[]{:S(2)}) %collective-permute-start) | collective-permute-done | bytes 245792 | tf_op jit(solution)/shard_map/ppermute | solution.py:141
  16.2 0.1 broadcast_in_dim.5.cos_ref
  16.3 0.0 copy-done.1
  16.3 0.7 %shard_map.29.u_ref = f32[3,80,256]{2,1,0:T(8,128)S(1)} custom-call(s32[1]{0:T(128)} %bitcast.parity_ref, f32[1]{0:T(128)S(6)} %copy.3.step_ref, f32[3,80,256]{2,1,0:T(8,128)S(1)} %copy-done.1, f32[3,80,256]{2,1,0:T(8,128)S(1)} %collective-permute-done.even_ref, f32[3,80,256]{2,1,0:T(8,128)S(1)} %collective-permute-done.1.odd_ref, ...), custom_call_target="tpu_custom_call" | custom-call | flops 4300800 | bytes 1720320 | tf_op jit(solution)/shard_map/pallas_call | solution.py:164
  16.9 5.7 %collective-permute-start.4 = (f32[3,80,256]{2,1,0:T(8,128)S(1)}, f32[3,80,256]{2,1,0:T(8,128)S(1)}, u32[]{:S(2)}, u32[]{:S(2)}) collective-permute-start(f32[3,80,256]{2,1,0:T(8,128)S(1)} %shard_map.29.u_ref), channel_id=1, source_target_pairs={{1,2},{2,1},{3,4},{4,3},{5,6},{6,5},{7,8},{8,7},{9,10},{10,9},{11,... | collective-permute-start | bytes 737288 | tf_op jit(solution)/shard_map/ppermute | solution.py:144
  22.6 1.9 %collective-permute-start.3 = (f32[3,80,256]{2,1,0:T(8,128)S(1)}, f32[3,80,256]{2,1,0:T(8,128)S(1)}, u32[]{:S(2)}, u32[]{:S(2)}) collective-permute-start(f32[3,80,256]{2,1,0:T(8,128)S(1)} %shard_map.29.u_ref), channel_id=1, source_target_pairs={{0,1},{1,0},{2,3},{3,2},{4,5},{5,4},{6,7},{7,6},{8,9},{9,8},{10,11... | collective-permute-start | bytes 737288 | tf_op jit(solution)/shard_map/ppermute | solution.py:141
  24.6 1.9 %collective-permute-start.5 = (f32[3,6,256]{2,1,0:T(8,128)S(1)}, f32[3,6,256]{2,1,0:T(8,128)S(1)}, u32[]{:S(2)}, u32[]{:S(2)}) collective-permute-start(f32[3,6,256]{2,1,0:T(8,128)S(1)} %pad_maximum_fusion.1), channel_id=1, source_target_pairs={{0,256},{256,0},{1,257},{257,1},{2,258},{258,2},{3,259},{259,3},{4... | collective-permute-start | bytes 55304 | tf_op jit(solution)/shard_map/ppermute | solution.py:148
  26.5 1.2 %collective-permute-done.5.edge_ref = f32[3,6,256]{2,1,0:T(8,128)S(1)} collective-permute-done((f32[3,6,256]{2,1,0:T(8,128)S(1)}, f32[3,6,256]{2,1,0:T(8,128)S(1)}, u32[]{:S(2)}, u32[]{:S(2)}) %collective-permute-start.5) | collective-permute-done | bytes 18464 | tf_op jit(solution)/shard_map/ppermute | solution.py:148
  27.7 1.5 %shard_map.30 = (f32[6,80,128]{2,1,0:T(8,128)S(1)}, f32[6,80,128]{2,1,0:T(8,128)S(1)}, f32[3,80,256]{2,1,0:T(8,128)S(1)}) custom-call(f32[1]{0:T(128)S(6)} %copy.3.step_ref, f32[3,80,256]{2,1,0:T(8,128)S(1)} %shard_map.29.u_ref, f32[3,6,256]{2,1,0:T(8,128)S(1)} %collective-permute-done.5.edge_ref, f32[80,128]{1,0:T(8,128)S(1)} %broadcast_in_dim.4.sin_ref, ...), custom_call_target="tpu_custom_call" | custom-call | flops 9216000 | bytes 737280 | tf_op jit(solution)/shard_map/pallas_call | solution.py:152
  29.1 1.9 %collective-permute-done.4.odd_ref = f32[3,80,256]{2,1,0:T(8,128)S(1)} collective-permute-done((f32[3,80,256]{2,1,0:T(8,128)S(1)}, f32[3,80,256]{2,1,0:T(8,128)S(1)}, u32[]{:S(2)}, u32[]{:S(2)}) %collective-permute-start.4) | collective-permute-done | bytes 245792 | tf_op jit(solution)/shard_map/ppermute | solution.py:144
  31.1 0.0 collective-permute-done.3.even_ref
  31.1 0.6 %shard_map.31.u_ref = f32[3,80,256]{2,1,0:T(8,128)S(1)} custom-call(s32[1]{0:T(128)} %bitcast.parity_ref, f32[1]{0:T(128)S(6)} %copy.3.step_ref, f32[3,80,256]{2,1,0:T(8,128)S(1)} %shard_map.29.u_ref, f32[3,80,256]{2,1,0:T(8,128)S(1)} %collective-permute-done.3.even_ref, f32[3,80,256]{2,1,0:T(8,128)S(1)} %collective-permute-done.4.odd_ref, ...), custom_call_target="tpu_custom_call" | custom-call | flops 4300800 | bytes 1720320 | tf_op jit(solution)/shard_map/pallas_call | solution.py:164
  31.7 5.7 %collective-permute-start.7 = (f32[3,80,256]{2,1,0:T(8,128)S(1)}, f32[3,80,256]{2,1,0:T(8,128)S(1)}, u32[]{:S(2)}, u32[]{:S(2)}) collective-permute-start(f32[3,80,256]{2,1,0:T(8,128)S(1)} %shard_map.31.u_ref), channel_id=1, source_target_pairs={{1,2},{2,1},{3,4},{4,3},{5,6},{6,5},{7,8},{8,7},{9,10},{10,9},{11,... | collective-permute-start | bytes 737288 | tf_op jit(solution)/shard_map/ppermute | solution.py:144
  37.4 1.9 %collective-permute-start.6 = (f32[3,80,256]{2,1,0:T(8,128)S(1)}, f32[3,80,256]{2,1,0:T(8,128)S(1)}, u32[]{:S(2)}, u32[]{:S(2)}) collective-permute-start(f32[3,80,256]{2,1,0:T(8,128)S(1)} %shard_map.31.u_ref), channel_id=1, source_target_pairs={{0,1},{1,0},{2,3},{3,2},{4,5},{5,4},{6,7},{7,6},{8,9},{9,8},{10,11... | collective-permute-start | bytes 737288 | tf_op jit(solution)/shard_map/ppermute | solution.py:141
  39.4 1.9 %collective-permute-start.8 = (f32[3,6,256]{2,1,0:T(8,128)S(1)}, f32[3,6,256]{2,1,0:T(8,128)S(1)}, u32[]{:S(2)}, u32[]{:S(2)}) collective-permute-start(f32[3,6,256]{2,1,0:T(8,128)S(1)} %pad_maximum_fusion.2), channel_id=1, source_target_pairs={{0,256},{256,0},{1,257},{257,1},{2,258},{258,2},{3,259},{259,3},{4... | collective-permute-start | bytes 55304 | tf_op jit(solution)/shard_map/ppermute | solution.py:148
  41.3 1.2 %collective-permute-done.8.edge_ref = f32[3,6,256]{2,1,0:T(8,128)S(1)} collective-permute-done((f32[3,6,256]{2,1,0:T(8,128)S(1)}, f32[3,6,256]{2,1,0:T(8,128)S(1)}, u32[]{:S(2)}, u32[]{:S(2)}) %collective-permute-start.8) | collective-permute-done | bytes 18464 | tf_op jit(solution)/shard_map/ppermute | solution.py:148
  42.5 1.5 %shard_map.32 = (f32[6,80,128]{2,1,0:T(8,128)S(1)}, f32[6,80,128]{2,1,0:T(8,128)S(1)}, f32[3,80,256]{2,1,0:T(8,128)S(1)}) custom-call(f32[1]{0:T(128)S(6)} %copy.3.step_ref, f32[3,80,256]{2,1,0:T(8,128)S(1)} %shard_map.31.u_ref, f32[3,6,256]{2,1,0:T(8,128)S(1)} %collective-permute-done.8.edge_ref, f32[80,128]{1,0:T(8,128)S(1)} %broadcast_in_dim.4.sin_ref, ...), custom_call_target="tpu_custom_call" | custom-call | flops 9216000 | bytes 737280 | tf_op jit(solution)/shard_map/pallas_call | solution.py:152
  44.0 1.3 %collective-permute-done.7.odd_ref = f32[3,80,256]{2,1,0:T(8,128)S(1)} collective-permute-done((f32[3,80,256]{2,1,0:T(8,128)S(1)}, f32[3,80,256]{2,1,0:T(8,128)S(1)}, u32[]{:S(2)}, u32[]{:S(2)}) %collective-permute-start.7) | collective-permute-done | bytes 245792 | tf_op jit(solution)/shard_map/ppermute | solution.py:144
  45.3 0.3 collective-permute-done.6.even_ref
  45.5 1.3 %shard_map.33 = f32[3,80,256]{2,1,0:T(8,128)} custom-call(s32[1]{0:T(128)} %bitcast.parity_ref, f32[1]{0:T(128)S(6)} %copy.3.step_ref, f32[3,80,256]{2,1,0:T(8,128)S(1)} %shard_map.31.u_ref, f32[3,80,256]{2,1,0:T(8,128)S(1)} %collective-permute-done.6.even_ref, f32[3,80,256]{2,1,0:T(8,128)S(1)} %collective-permute-done.7.odd_ref, ...), custom_call_target="tpu_custom_call" | custom-call | flops 4300800 | bytes 1720320 | tf_op jit(solution)/shard_map/pallas_call | solution.py:164
  (6 shorter events, 0.1 us)
Async XLA Ops:
  0.0 15.2 %collective-permute-start.1 = (f32[3,80,256]{2,1,0:T(8,128)}, f32[3,80,256]{2,1,0:T(8,128)S(1)}, u32[]{:S(2)}, u32[]{:S(2)}) collective-permute-start(f32[3,80,256]{2,1,0:T(8,128)} %first_ref.5), channel_id=1, source_target_pairs={{1,2},{2,1},{3,4},{4,3},{5,6},{6,5},{7,8},{8,7},{9,10},{10,9},{11,... | collective-permute-start | bytes 737288 | tf_op jit(solution)/shard_map/ppermute | solution.py:144
  6.7 9.5 %collective-permute-start = (f32[3,80,256]{2,1,0:T(8,128)}, f32[3,80,256]{2,1,0:T(8,128)S(1)}, u32[]{:S(2)}, u32[]{:S(2)}) collective-permute-start(f32[3,80,256]{2,1,0:T(8,128)} %first_ref.5), channel_id=1, source_target_pairs={{0,1},{1,0},{2,3},{3,2},{4,5},{5,4},{6,7},{7,6},{8,9},{9,8},{10,11... | collective-permute-start | bytes 737288 | tf_op jit(solution)/shard_map/ppermute | solution.py:141
  9.4 3.1 %collective-permute-start.2 = (f32[3,6,256]{2,1,0:T(8,128)S(1)}, f32[3,6,256]{2,1,0:T(8,128)S(1)}, u32[]{:S(2)}, u32[]{:S(2)}) collective-permute-start(f32[3,6,256]{2,1,0:T(8,128)S(1)} %pad_maximum_fusion), channel_id=1, source_target_pairs={{0,256},{256,0},{1,257},{257,1},{2,258},{258,2},{3,259},{259,3},{4... | collective-permute-start | bytes 55304 | tf_op jit(solution)/shard_map/ppermute | solution.py:148
  12.6 1.0 %copy-start = (f32[3,80,256]{2,1,0:T(8,128)S(1)}, f32[3,80,256]{2,1,0:T(8,128)}, u32[]{:S(2)}) copy-start(f32[3,80,256]{2,1,0:T(8,128)} %first_ref.5) | copy-start | bytes 737284
  13.5 2.7 %copy-start.1 = (f32[3,80,256]{2,1,0:T(8,128)S(1)}, f32[3,80,256]{2,1,0:T(8,128)}, u32[]{:S(2)}) copy-start(f32[3,80,256]{2,1,0:T(8,128)} %first_ref.5) | copy-start | bytes 737284
  16.9 14.1 %collective-permute-start.4 = (f32[3,80,256]{2,1,0:T(8,128)S(1)}, f32[3,80,256]{2,1,0:T(8,128)S(1)}, u32[]{:S(2)}, u32[]{:S(2)}) collective-permute-start(f32[3,80,256]{2,1,0:T(8,128)S(1)} %shard_map.29.u_ref), channel_id=1, source_target_pairs={{1,2},{2,1},{3,4},{4,3},{5,6},{6,5},{7,8},{8,7},{9,10},{10,9},{11,... | collective-permute-start | bytes 737288 | tf_op jit(solution)/shard_map/ppermute | solution.py:144
  22.6 8.5 %collective-permute-start.3 = (f32[3,80,256]{2,1,0:T(8,128)S(1)}, f32[3,80,256]{2,1,0:T(8,128)S(1)}, u32[]{:S(2)}, u32[]{:S(2)}) collective-permute-start(f32[3,80,256]{2,1,0:T(8,128)S(1)} %shard_map.29.u_ref), channel_id=1, source_target_pairs={{0,1},{1,0},{2,3},{3,2},{4,5},{5,4},{6,7},{7,6},{8,9},{9,8},{10,11... | collective-permute-start | bytes 737288 | tf_op jit(solution)/shard_map/ppermute | solution.py:141
  24.6 3.1 %collective-permute-start.5 = (f32[3,6,256]{2,1,0:T(8,128)S(1)}, f32[3,6,256]{2,1,0:T(8,128)S(1)}, u32[]{:S(2)}, u32[]{:S(2)}) collective-permute-start(f32[3,6,256]{2,1,0:T(8,128)S(1)} %pad_maximum_fusion.1), channel_id=1, source_target_pairs={{0,256},{256,0},{1,257},{257,1},{2,258},{258,2},{3,259},{259,3},{4... | collective-permute-start | bytes 55304 | tf_op jit(solution)/shard_map/ppermute | solution.py:148
  31.7 13.5 %collective-permute-start.7 = (f32[3,80,256]{2,1,0:T(8,128)S(1)}, f32[3,80,256]{2,1,0:T(8,128)S(1)}, u32[]{:S(2)}, u32[]{:S(2)}) collective-permute-start(f32[3,80,256]{2,1,0:T(8,128)S(1)} %shard_map.31.u_ref), channel_id=1, source_target_pairs={{1,2},{2,1},{3,4},{4,3},{5,6},{6,5},{7,8},{8,7},{9,10},{10,9},{11,... | collective-permute-start | bytes 737288 | tf_op jit(solution)/shard_map/ppermute | solution.py:144
  37.4 8.1 %collective-permute-start.6 = (f32[3,80,256]{2,1,0:T(8,128)S(1)}, f32[3,80,256]{2,1,0:T(8,128)S(1)}, u32[]{:S(2)}, u32[]{:S(2)}) collective-permute-start(f32[3,80,256]{2,1,0:T(8,128)S(1)} %shard_map.31.u_ref), channel_id=1, source_target_pairs={{0,1},{1,0},{2,3},{3,2},{4,5},{5,4},{6,7},{7,6},{8,9},{9,8},{10,11... | collective-permute-start | bytes 737288 | tf_op jit(solution)/shard_map/ppermute | solution.py:141
  39.4 3.1 %collective-permute-start.8 = (f32[3,6,256]{2,1,0:T(8,128)S(1)}, f32[3,6,256]{2,1,0:T(8,128)S(1)}, u32[]{:S(2)}, u32[]{:S(2)}) collective-permute-start(f32[3,6,256]{2,1,0:T(8,128)S(1)} %pad_maximum_fusion.2), channel_id=1, source_target_pairs={{0,256},{256,0},{1,257},{257,1},{2,258},{258,2},{3,259},{259,3},{4... | collective-permute-start | bytes 55304 | tf_op jit(solution)/shard_map/ppermute | solution.py:148
